TPU v7x, 256 devices: a whole 4x4x8 slice. The times are simulated.
256 devices in a mesh: seq: 64 (over z, x, core), head: 4 (over y).
Axes of the slice: x: 4, y: 4, z: 8, core: 2. Of those that a mesh axis runs over, the one named last changes fastest.
Arguments:
- queries: bfloat16 [32768, 4096], P(('seq', 'head')), may hold values from -6 to 6
- keys: bfloat16 [32768, 4096], P(('seq', 'head')), may hold values from -6 to 6
- values: bfloat16 [32768, 4096], P(('seq', 'head')), may hold values from -128 to 128
- out_grad: bfloat16 [32768, 4096], P(('seq', 'head')), may hold values from -16 to 16
- doc_lengths: int32 [8], replicated, may hold values from 1 to 16384, 32768 in all
Outputs:
- attn_out: bfloat16 [32768, 4096], P(('seq', 'head'))
- grad_queries: bfloat16 [32768, 4096], P(('seq', 'head'))
- grad_keys: bfloat16 [32768, 4096], P(('seq', 'head'))
- grad_values: bfloat16 [32768, 4096], P(('seq', 'head'))
Inputs may be any that keep to these rules, and one draw needn't show every extreme that they name: `doc_lengths`: the lengths sum to 32768; the longest is exactly 16384.
All inputs are finite; a program needn't handle non-finite values.
Results may differ from a plain program's by a relative error of at most 0.011.
Values may be sent and summed in bfloat16 or wider, within the bound.
A program may use at most 128 MiB of HBM per device.

v0:
```python
import jax
import jax.numpy as jnp
from jax import lax
from jax.sharding import PartitionSpec as P

DH = 128


def prefix(value, axis, join, neutral):
    count, mine = (lax.axis_size(axis), lax.axis_index(axis))
    pieces = jax.tree.map(lambda part: lax.all_gather(part, axis), value)
    so_far = jax.tree.map(
        lambda part, zero: jnp.full_like(part, 0) + jnp.asarray(zero, part.dtype), value, neutral
    )

    def lap(position, so_far):
        longer = join(so_far, jax.tree.map(lambda part: part[position], pieces))
        return jax.tree.map(lambda new, old: jnp.where(position < mine, new, old), longer, so_far)

    return lax.fori_loop(0, count - 1, lap, so_far)


def prefix_2(array, axis, join, neutral):
    count = lax.axis_size(axis)
    place = lax.axis_index(axis)
    ahead = count - 1 - place
    gathered = jax.tree.map(
        lambda a, kind: lax.all_gather(a.astype(kind), axis), array, (jnp.bfloat16, jnp.bfloat16)
    )
    state = jax.tree.map(lambda a, e: jnp.zeros_like(a) + jnp.asarray(e, a.dtype), array, neutral)

    def one(lap, state):
        source = count - 1 - lap
        return join(
            state,
            jax.tree.map(
                lambda a, own: lax.dynamic_index_in_dim(a, source, 0, False).astype(own.dtype),
                gathered,
                array,
            ),
        )

    return lax.fori_loop(0, ahead, one, state)


def feature(array):
    wide = array.astype(jnp.float32)
    return jnp.where(wide > 0, wide + 1.0, jnp.exp(jnp.minimum(wide, 0.0)))


def slope(array):
    wide = array.astype(jnp.float32)
    return jnp.where(wide > 0, 1.0, jnp.exp(jnp.minimum(wide, 0.0)))


def doc_index(doc_ends, where):
    return jnp.sum((jnp.asarray(where)[..., None] >= doc_ends).astype(jnp.int32), axis=-1)


def linked(earlier, later):
    return (later[0] + (1.0 - later[1]) * earlier[0], jnp.maximum(earlier[1], later[1]))


def local(queries, keys, values, out_grad, doc_lengths):
    shared = (
        lax.all_to_all(queries, "head", split_axis=1, concat_axis=0, tiled=True),
        lax.all_to_all(keys, "head", split_axis=1, concat_axis=0, tiled=True),
        lax.all_to_all(values, "head", split_axis=1, concat_axis=0, tiled=True),
        lax.all_to_all(out_grad, "head", split_axis=1, concat_axis=0, tiled=True),
    )
    block_len = shared[0].shape[0]
    head_count = shared[0].shape[1] // DH
    query_rows = shared[0].reshape(block_len, head_count, DH)
    key_rows = shared[1].reshape(block_len, head_count, DH)
    value_rows = shared[2].reshape(block_len, head_count, DH)
    grad_rows = shared[3].reshape(block_len, head_count, DH)
    block_index = lax.axis_index("seq")
    doc_ends = jnp.cumsum(doc_lengths)
    block_start = block_index * block_len
    within = jnp.arange(block_len, dtype=jnp.int32)
    doc_of = doc_index(doc_ends, block_start + within)
    doc_first = doc_of[0]
    doc_last = doc_of[block_len - 1]
    before = doc_index(doc_ends, block_start - 1)
    doc_after = doc_index(doc_ends, block_start + block_len)
    visible = (within[:, None] >= within[None, :]) & (doc_of[:, None] == doc_of[None, :])
    head_rows = (doc_of == doc_first)[:, None, None]
    tail_rows = (doc_of == doc_last)[:, None, None]
    tile_rows = 256
    tile_count = block_len // tile_rows
    feat_query = feature(query_rows).astype(jnp.bfloat16)
    feat_key = feature(key_rows).astype(jnp.bfloat16)
    zero_bf = jnp.zeros((), jnp.bfloat16)
    tail_state = jnp.einsum(
        "shd,she->hde",
        jnp.where(tail_rows, feat_key, zero_bf),
        value_rows,
        preferred_element_type=jnp.float32,
    )
    reset_flag = (doc_last != before).astype(jnp.float32)
    carried, _ = prefix(
        (tail_state, reset_flag),
        "seq",
        linked,
        (jnp.zeros_like(tail_state), jnp.zeros((), jnp.float32)),
    )
    incoming = jnp.where(doc_first == before, carried, 0.0).astype(jnp.bfloat16)
    score_tiles = []
    normed_tiles = []
    grad_att_tiles = []
    for tile in range(tile_count):
        first = tile * tile_rows
        last = first + tile_rows
        query_tile = feat_query[first:last]
        tile_scores = jnp.einsum(
            "thd,shd->hts", query_tile, feat_key[:last], preferred_element_type=jnp.float32
        )
        tile_scores = jnp.where(visible[first:last, :last][None], tile_scores, 0.0).astype(
            jnp.bfloat16
        )
        attended = jnp.einsum(
            "hts,she->the", tile_scores, value_rows[:last], preferred_element_type=jnp.float32
        )
        attended = attended + jnp.where(
            head_rows[first:last],
            jnp.einsum("thd,hde->the", query_tile, incoming, preferred_element_type=jnp.float32),
            0.0,
        )
        inv_rms = lax.rsqrt(jnp.mean(attended * attended, axis=-1, keepdims=True) + 1e-05)
        normed = attended * inv_rms
        grad_out = grad_rows[first:last].astype(jnp.float32)
        grad_att_tile = (
            (grad_out - normed * jnp.mean(grad_out * normed, axis=-1, keepdims=True)) * inv_rms
        ).astype(jnp.bfloat16)
        score_tiles.append(tile_scores)
        normed_tiles.append(normed.astype(jnp.bfloat16))
        grad_att_tiles.append(grad_att_tile)
    out_block = jnp.concatenate(normed_tiles, axis=0).reshape(block_len, head_count * DH)
    grad_att = jnp.concatenate(grad_att_tiles, axis=0)
    attn_out = lax.all_to_all(out_block, "head", split_axis=0, concat_axis=1, tiled=True)
    head_sum = jnp.einsum(
        "thd,the->hde",
        jnp.where(head_rows, feat_query, zero_bf),
        grad_att,
        preferred_element_type=jnp.float32,
    )
    reset_back = (doc_first != doc_after).astype(jnp.float32)
    future, _ = prefix_2(
        (head_sum, reset_back),
        "seq",
        linked,
        (jnp.zeros_like(head_sum), jnp.zeros((), jnp.float32)),
    )
    outgoing = jnp.where(doc_last == doc_after, future, 0.0).astype(jnp.bfloat16)
    grad_fk = jnp.zeros((block_len, head_count, DH), jnp.float32)
    grad_fv = jnp.zeros((block_len, head_count, DH), jnp.float32)
    grad_fq_tiles = []
    for tile in range(tile_count):
        first = tile * tile_rows
        last = first + tile_rows
        grad_tile = grad_att_tiles[tile]
        tile_grads = jnp.einsum(
            "the,she->hts", grad_tile, value_rows[:last], preferred_element_type=jnp.float32
        )
        tile_grads = jnp.where(visible[first:last, :last][None], tile_grads, 0.0).astype(
            jnp.bfloat16
        )
        grad_fq_tile = jnp.einsum(
            "hts,shd->thd", tile_grads, feat_key[:last], preferred_element_type=jnp.float32
        )
        grad_fq_tile = grad_fq_tile + jnp.where(
            head_rows[first:last],
            jnp.einsum("the,hde->thd", grad_tile, incoming, preferred_element_type=jnp.float32),
            0.0,
        )
        grad_fq_tiles.append(grad_fq_tile)
        grad_fk = grad_fk.at[:last].add(
            jnp.einsum(
                "hts,thd->shd",
                tile_grads,
                feat_query[first:last],
                preferred_element_type=jnp.float32,
            )
        )
        grad_fv = grad_fv.at[:last].add(
            jnp.einsum(
                "hts,the->she", score_tiles[tile], grad_tile, preferred_element_type=jnp.float32
            )
        )
    grad_fq = jnp.concatenate(grad_fq_tiles, axis=0)
    grad_fk = grad_fk + jnp.where(
        tail_rows,
        jnp.einsum("she,hde->shd", value_rows, outgoing, preferred_element_type=jnp.float32),
        0.0,
    )
    grad_fv = grad_fv + jnp.where(
        tail_rows,
        jnp.einsum("shd,hde->she", feat_key, outgoing, preferred_element_type=jnp.float32),
        0.0,
    )
    grad_query = (
        (grad_fq * slope(query_rows)).astype(jnp.bfloat16).reshape(block_len, head_count * DH)
    )
    grad_key = (grad_fk * slope(key_rows)).astype(jnp.bfloat16).reshape(block_len, head_count * DH)
    grad_value = grad_fv.astype(jnp.bfloat16).reshape(block_len, head_count * DH)
    grad_queries, grad_keys, grad_values = (
        lax.all_to_all(grad_query, "head", split_axis=0, concat_axis=1, tiled=True),
        lax.all_to_all(grad_key, "head", split_axis=0, concat_axis=1, tiled=True),
        lax.all_to_all(grad_value, "head", split_axis=0, concat_axis=1, tiled=True),
    )
    return (attn_out, grad_queries, grad_keys, grad_values)


def solution(mesh):
    placed = (
        P(("seq", "head"), None),
        P(("seq", "head"), None),
        P(("seq", "head"), None),
        P(("seq", "head"), None),
        P(),
    )
    return jax.shard_map(
        local,
        mesh=mesh,
        in_specs=placed,
        out_specs=(
            P(("seq", "head"), None),
            P(("seq", "head"), None),
            P(("seq", "head"), None),
            P(("seq", "head"), None),
        ),
        check_vma=False,
    )
```

profile of v0, /device:TPU:1, one launch (start us, length us, event | category | flops | bytes accessed | tf_op | source)
XLA Modules:
  0.0 779.7 jit_solution(12176665650693809135)
XLA Ops:
  7.2 2.4 copy.285
  9.5 5.1 all-to-all-start.1
  15.9 12.3 %all-to-all-done.1 = bf16[128,4,1024]{2,0,1:T(8,128)(2,1)S(1)} async-done(((bf16[128,4,1024]{2,0,1:T(8,128)(2,1)}), bf16[128,4,1024]{2,0,1:T(8,128)(2,1)S(1)}, u32[]{:S(2)}, u32[]{:S(2)}) %all-to-all-start.1) | async-done | bytes 1048608 | tf_op jit(solution)/shard_map/all_to_all | solution.py:67
  28.2 3.5 all-to-all-start.2
  33.8 2.2 fusion.11
  36.3 7.7 all-to-all-done.2
  44.3 1.8 broadcast_select_fusion
  48.6 4.4 all-to-all-start
  56.6 2.3 copy.283
  60.1 134.8 %all-reduce.2 = f32[64]{0:T(128)S(1)} all-reduce(f32[64]{0:T(128)S(1)} %dynamic-update-slice.10), channel_id=1, replica_groups=mesh['seq'=64,'head'=4] {'seq'}, use_global_device_ids=true, to_apply=%add.2 | all-reduce | flops 64 | bytes 512
  194.9 4.8 all-to-all-start.4
  199.7 2.7 fusion.2
  207.8 2.1 copy.198
  211.9 2.5 slice_convert_fusion.1
  216.5 2.1 copy.212
  218.6 2.5 copy.250
  221.4 2.8 bitcast_select_fusion
  229.3 1.7 convolution_bitcast_fusion
  231.0 168.2 %while.35 = (s32[]{:T(128)}, f32[8,128,128]{2,1,0:T(8,128)S(1)}, s32[]{:T(128)}, f32[64,8,128,128]{3,2,1,0:T(8,128)}, f32[64]{0:T(128)S(1)}, /*index=5*/s32[]{:T(128)}, f32[1]{0:T(128)}, s32[]{:T(128)}) while((s32[]{:T(128)}, f32[8,128,128]{2,1,0:T(8,128)S(1)}, s32[]{:T(128)}, f32[64,8,128,128]{3,2,1,0:T(8,128)}, f32[64]{0:T(128)S(1)}, ...), condition=%wide.region_4.5_spmd.clone, body=%wide.region_3.4_spmd.clone.sunk | while | flops 524293 | bytes 1573001 | solution.py:20
  399.3 2.0 multiply_reduce_fusion.3
  403.3 2.1 multiply_convert_fusion
  406.7 1.5 select_convert_fusion.2
  410.5 2.5 copy.201
  416.4 2.7 copy.208
  419.1 2.9 pad_maximum_fusion
  422.0 2.9 copy.236
  424.9 3.4 fusion.7
  428.3 4.3 all-to-all-start.5
  435.9 129.0 %all-reduce.3 = bf16[64]{0:T(256)(128)(2,1)S(1)} all-reduce(bf16[64]{0:T(256)(128)(2,1)S(1)} %dynamic-update-slice.11), channel_id=1, replica_groups=mesh['seq'=64,'head'=4] {'seq'}, use_global_device_ids=true, to_apply=%add.3 | all-reduce | flops 64 | bytes 256
  564.8 3.4 copy.252
  568.3 3.0 copy.237
  571.3 1.6 copy.192
  573.0 2.3 all_to_all.105
  575.3 2.5 convolution_bitcast_fusion.1
  577.8 1.9 fusion.52
  579.7 4.6 all-to-all-start.3
  584.3 150.9 %while.34 = (s32[]{:T(128)}, f32[8,128,128]{2,1,0:T(8,128)S(1)}, s32[]{:T(128)}, bf16[64,8,128,128]{3,2,1,0:T(8,128)(2,1)}, bf16[64]{0:T(256)(128)(2,1)S(1)}, /*...) while((s32[]{:T(128)}, f32[8,128,128]{2,1,0:T(8,128)S(1)}, s32[]{:T(128)}, ...), condition=%wide.region_11.12_spmd, body=%wide.region_10.11_spmd.sunk | while | flops 393223 | bytes 1310893 | solution.py:43
  735.2 3.4 fusion.12
  738.6 2.1 all_to_all.119
  740.7 2.4 copy.221
  743.1 4.4 all-to-all-start.7
  747.6 1.7 convolution_bitcast_fusion.2
  753.1 5.2 all-to-all-done.7
  758.3 3.5 all-to-all-start.6
  761.8 2.3 copy.242
  764.1 1.6 copy.193
  767.1 2.3 copy.224
  769.3 2.2 all-to-all-done.6
  (386 shorter events, 278.4 us)
Async XLA Ops:
  7.2 7.5 copy-start.29
  9.5 6.2 copy-start.33
  9.5 18.6 %all-to-all-start.1 = ((bf16[128,4,1024]{2,0,1:T(8,128)(2,1)}), bf16[128,4,1024]{2,0,1:T(8,128)(2,1)S(1)}, u32[]{:S(2)}, u32[]{:S(2)}) async-start(bf16[128,4,1024]{2,0,1:T(8,128)(2,1)} %bitcast.161), calls=%async_computation.1 | async-start | bytes 2097152 | tf_op jit(solution)/shard_map/all_to_all | solution.py:67
  28.2 15.8 %all-to-all-start.2 = ((bf16[128,4,1024]{2,0,1:T(8,128)(2,1)}), bf16[128,4,1024]{2,0,1:T(8,128)(2,1)S(1)}, u32[]{:S(2)}, u32[]{:S(2)}) async-start(bf16[128,4,1024]{2,0,1:T(8,128)(2,1)} %bitcast.160), calls=%async_computation.2 | async-start | bytes 2097152 | tf_op jit(solution)/shard_map/all_to_all | solution.py:68
  31.7 199.3 %all-gather.5.cloned.1.call-start = ((), (), s32[]{:S(2)}) async-start(), calls=%async_computation.8 | async-start | bytes 34078720 | tf_op jit(solution)/shard_map/all_gather | solution.py:11
  44.0 2.0 copy-start.11
  46.1 1.5 copy-start.30
  48.6 10.3 %copy-start.34 = (u32[256]{0:T(256)S(1)}, u32[256]{0:T(256)}, u32[]{:S(2)}) copy-start(u32[256]{0:T(256)} %constant.223) | copy-start | bytes 3076
  48.6 146.3 %all-to-all-start = ((bf16[128,4,1024]{2,0,1:T(8,128)(2,1)}), bf16[128,4,1024]{2,0,1:T(8,128)(2,1)}, u32[]{:S(2)}, u32[]{:S(2)}) async-start(bf16[128,4,1024]{2,0,1:T(8,128)(2,1)} %bitcast.162), calls=%async_computation | async-start | bytes 2097152 | tf_op jit(solution)/shard_map/all_to_all | solution.py:66
  56.5 170.5 %copy-start.31 = (pred[256,512]{1,0:T(8,128)(4,1)}, pred[256,512]{1,0:T(8,128)(4,1)S(1)}, u32[]{:S(2)}) copy-start(pred[256,512]{1,0:T(8,128)(4,1)S(1)} %slice.160) | copy-start | bytes 393220
  194.9 17.0 %all-to-all-start.4 = ((bf16[128,4,1024]{2,0,1:T(8,128)(2,1)}), bf16[128,4,1024]{2,0,1:T(8,128)(2,1)}, u32[]{:S(2)}, u32[]{:S(2)}) async-start(bf16[128,4,1024]{2,0,1:T(8,128)(2,1)} %bitcast.191), calls=%async_computation.4 | async-start | bytes 2097152 | tf_op jit(solution)/shard_map/all_to_all | solution.py:69
  199.7 384.5 %all-gather.7.cloned.1.call-start = ((), (), s32[]{:S(2)}) async-start(), calls=%async_computation.9 | async-start | bytes 17039360 | tf_op jit(solution)/shard_map/all_gather | solution.py:28
  205.6 193.7 %copy-start.4 = (bf16[256,8,128]{0,2,1:T(8,128)(2,1)}, bf16[256,8,128]{0,2,1:T(8,128)(2,1)S(1)}, u32[]{:S(2)}) copy-start(bf16[256,8,128]{0,2,1:T(8,128)(2,1)S(1)} %copy.211) | copy-start | bytes 1572868
  211.9 3.6 copy-start.27
  218.6 2.5 copy-start.20
  221.1 3.1 copy-start.18
  221.4 4.3 copy-start.24
  224.2 2.9 copy-start.12
  224.7 1.0 copy-start
  227.9 1.3 copy-start.6
  399.2 2.1 copy-start.2
  399.3 2.7 copy-start.13
  399.3 2.7 copy-start.22
  401.3 1.3 copy-start.3
  403.3 2.1 copy-start.28
  405.4 3.3 copy-start.17
  405.4 9.1 %copy-start.15 = (bf16[256,8,128]{2,0,1:T(8,128)(2,1)}, bf16[256,8,128]{2,0,1:T(8,128)(2,1)S(1)}, u32[]{:S(2)}) copy-start(bf16[256,8,128]{2,0,1:T(8,128)(2,1)S(1)} %get-tuple-element.302) | copy-start | bytes 1572868
  406.7 1.6 copy-start.19
  408.2 1.0 copy-start.21
  409.2 3.8 copy-start.32
  413.8 1.4 copy-start.8
  416.4 2.7 copy-start.23
  428.3 151.4 %all-to-all-start.5 = ((bf16[4,128,1024]{2,1,0:T(8,128)(2,1)}), bf16[4,128,1024]{2,1,0:T(8,128)(2,1)}, u32[]{:S(2)}, u32[]{:S(2)}) async-start(bf16[4,128,1024]{2,1,0:T(8,128)(2,1)} %fusion.7), calls=%async_computation.5 | async-start | bytes 2097152 | tf_op jit(solution)/shard_map/all_to_all | solution.py:207
  568.3 3.0 copy-start.25
  568.3 3.0 copy-start.26
  571.3 4.0 copy-start.1
  575.3 2.5 copy-start.7
  575.3 2.5 copy-start.16
  579.7 163.5 %all-to-all-start.3 = ((bf16[4,128,1024]{2,1,0:T(8,128)(2,1)}), bf16[4,128,1024]{2,1,0:T(8,128)(2,1)}, u32[]{:S(2)}, u32[]{:S(2)}) async-start(bf16[4,128,1024]{2,1,0:T(8,128)(2,1)} %all_to_all.105), calls=%async_computation.3 | async-start | bytes 2097152 | tf_op jit(solution)/shard_map/all_to_all | solution.py:140
  740.7 6.8 copy-start.5
  743.1 6.1 copy-start.14
  743.1 15.2 %all-to-all-start.7 = ((bf16[4,128,1024]{1,2,0:T(8,128)(2,1)}), bf16[4,128,1024]{1,2,0:T(8,128)(2,1)}, u32[]{:S(2)}, u32[]{:S(2)}) async-start(bf16[4,128,1024]{1,2,0:T(8,128)(2,1)} %copy.221), calls=%async_computation.7 | async-start | bytes 2097152 | tf_op jit(solution)/shard_map/all_to_all | solution.py:209
  747.6 1.9 copy-start.9
  749.5 1.6 copy-start.10
  758.3 13.2 %all-to-all-start.6 = ((bf16[4,128,1024]{1,2,0:T(8,128)(2,1)}), bf16[4,128,1024]{1,2,0:T(8,128)(2,1)S(1)}, u32[]{:S(2)}, u32[]{:S(2)}) async-start(bf16[4,128,1024]{1,2,0:T(8,128)(2,1)} %copy.216), calls=%async_computation.6 | async-start | bytes 2097152 | tf_op jit(solution)/shard_map/all_to_all | solution.py:208
Sparse Core Ops, SparseCore 0:
  47.7 147.5 all-gather.4
  406.8 98.5 all-gather.6
where the time goes:
time: 791 us; the launch traced here: 780 us
  blocking collectives  264 us (33%)
  other arithmetic  189 us (24%)
  local copies, waits for them, and re-layouts  138 us (17%)
  loops' own time  80.1 us (10%)
  starting transfers between devices  34.7 us (4%)
  waiting for transfers between devices  27.5 us (3%)
  matrix products  26.3 us (3%)
  between operations  19.7 us (2%)
    unnamed x2, blocking collectives  264 us
    select_n x63, other arithmetic, lap(): jnp.where(position < mine, new, old)  93.2 us
    add x62, other arithmetic, linked(): later[0] + (1.0 - later[1]) * earlier[0]  72 us
    another operation x1, loops' own time, prefix_2(): return lax.fori_loop(0, ahead, one, state)  42.3 us
    another operation x1, loops' own time, prefix(): return lax.fori_loop(0, count - 1, lap, so_far)  37.8 us
    dynamic_slice x63, local copies, waits for them, and re-layouts, lap(): longer = join(so_far, jax.tree.map(lambda part: part[position], pieces))  37.2 us
    dynamic_slice x62, local copies, waits for them, and re-layouts, one(): lax.dynamic_index_in_dim(a, source, 0, False).astype(own.dtype)  36.6 us
    unnamed x88, local copies, waits for them, and re-layouts  23.2 us
  transfers between devices with their start and end apart: 10, of which 4 were waited for; matrix products, arithmetic and copies ran while one was open for 26% of the time, Pallas kernels for 0%

commit v1 on v0

v1 whole, which is shorter than its diff:
```python
import functools

import jax
import jax.numpy as jnp
from jax import lax
from jax.experimental import pallas as pl
from jax.experimental.pallas import tpu as pltpu
from jax.sharding import PartitionSpec as P

DH = 128
DOC_MOST = 16384
UNROLL = 4
MESH = pl.DeviceIdType.MESH
F32 = jnp.float32
BF16 = jnp.bfloat16


def mm(a, b, ca, cb):
    return lax.dot_general(a, b, (((ca,), (cb,)), ((), ())), preferred_element_type=F32)


def feature(x):
    return jnp.where(x > 0, x + 1.0, jnp.exp(jnp.minimum(x, 0.0)))


def slope(x):
    return jnp.where(x > 0, 1.0, jnp.exp(jnp.minimum(x, 0.0)))


def kernel(
    cfg,
    len_ref,
    q_hbm,
    k_hbm,
    v_hbm,
    g_hbm,
    o_hbm,
    gq_hbm,
    gk_hbm,
    gv_hbm,
    q_ref,
    k_ref,
    v_ref,
    g_ref,
    o_ref,
    gq_ref,
    gk_ref,
    gv_ref,
    fq_ref,
    fk_ref,
    sc_ref,
    ga_ref,
    att_ref,
    gfk_ref,
    gfv_ref,
    state_out,
    state_in,
    total_out,
    total_in,
    visible_ref,
    rows_ref,
    weight_ref,
    send_sem,
    recv_sem,
    zsend_sem,
    zrecv_sem,
    load_sem,
):
    heads, plane_seq, head_axis, planes, reach = cfg
    groups = heads // UNROLL
    seq = lax.axis_index("seq")
    place = lax.axis_index("head")
    z = seq // plane_seq
    mine = (seq % plane_seq) * head_axis + place
    block = z * heads + mine

    def peer(p):
        return (z * plane_seq + p // head_axis, p % head_axis)

    def plane_peer(other):
        return (other * plane_seq + seq % plane_seq, place)

    def cols(h):
        return pl.ds(pl.multiple_of(h * DH, DH), DH)

    loads = [
        pltpu.make_async_copy(src, dst, load_sem.at[n])
        for n, (src, dst) in enumerate(
            ((k_hbm, k_ref), (v_hbm, v_ref), (q_hbm, q_ref), (g_hbm, g_ref))
        )
    ]
    for load in loads:
        load.start()

    barrier = pltpu.get_barrier_semaphore()

    def greet(n, carry):
        pl.semaphore_signal(
            barrier, inc=1, device_id=peer((mine + n) % heads), device_id_type=MESH
        )
        return carry

    lax.fori_loop(1, heads, greet, 0)
    for n in range(1, planes):
        pl.semaphore_signal(
            barrier, inc=1, device_id=plane_peer((z + n) % planes), device_id_type=MESH
        )

    ends = []
    end = jnp.int32(0)
    for n in range(len_ref.shape[0]):
        end = end + len_ref[n]
        ends.append(end)

    def doc_of(where):
        return sum([(where >= e).astype(jnp.int32) for e in ends])

    def equal(a, b):
        return jnp.where(a == b, 1.0, 0.0).astype(F32)

    start = block * DH
    row_doc = doc_of(start + lax.broadcasted_iota(jnp.int32, (DH, DH), 0))
    col_doc = doc_of(start + lax.broadcasted_iota(jnp.int32, (DH, DH), 1))
    causal = lax.broadcasted_iota(jnp.int32, (DH, DH), 0) >= lax.broadcasted_iota(
        jnp.int32, (DH, DH), 1
    )
    visible_ref[...] = jnp.where(causal & (row_doc == col_doc), 1.0, 0.0).astype(F32)
    rows_ref[0] = jnp.where(row_doc == doc_of(start), 1.0, 0.0).astype(F32)
    rows_ref[1] = jnp.where(row_doc == doc_of(start + DH - 1), 1.0, 0.0).astype(F32)

    plane_start = z * (heads * DH)
    plane_first = doc_of(plane_start)
    plane_last = doc_of(plane_start + heads * DH - 1)

    def weigh(i, carry):
        begin = plane_start + i * DH
        before, first = doc_of(begin - 1), doc_of(begin)
        last, after = doc_of(begin + DH - 1), doc_of(begin + DH)
        weight_ref[0, i] = equal(last, plane_last)
        weight_ref[1, i] = equal(last, before)
        weight_ref[2, i] = equal(first, before)
        weight_ref[3, i] = equal(first, plane_first)
        weight_ref[4, i] = equal(first, after)
        weight_ref[5, i] = equal(last, after)
        return carry

    lax.fori_loop(0, heads, weigh, 0)

    def remote(stage, slot, target_slot, p):
        return pltpu.make_async_remote_copy(
            src_ref=state_out.at[stage, slot],
            dst_ref=state_in.at[stage, target_slot],
            send_sem=send_sem.at[stage, slot],
            recv_sem=recv_sem.at[stage, target_slot],
            device_id=peer(p),
            device_id_type=MESH,
        )

    def send(stage, p):
        remote(stage, p, mine, p).start()

    def receive(stage, p):
        remote(stage, p, p, p).wait_recv()

    def to_own(stage):
        state_in[stage, mine] = state_out[stage, mine]

    def forward_state(kk):
        h = (mine + kk) % heads
        fk = feature(k_ref[:, cols(h)].astype(F32))
        fk_ref[h] = fk.astype(BF16)
        masked = (fk * rows_ref[1]).astype(BF16)
        state_out[0, h] = mm(masked, v_ref[:, cols(h)], 0, 0).astype(BF16)

    loads[0].wait()
    loads[1].wait()
    for j in range(UNROLL):
        forward_state(1 + j)
    pl.semaphore_wait(barrier, heads - 1 + planes - 1)

    def forward_lap(it, carry):
        for j in range(UNROLL):
            send(0, (mine + it * UNROLL + 1 + j) % heads)
        for j in range(UNROLL):
            forward_state((it + 1) * UNROLL + 1 + j)
        return carry

    lax.fori_loop(0, groups - 1, forward_lap, 0)
    for j in range(UNROLL - 1):
        send(0, (mine + (groups - 1) * UNROLL + 1 + j) % heads)
    to_own(0)

    loads[2].wait()

    def local_lap(it, carry):
        for j in range(UNROLL):
            h = it * UNROLL + j
            fq = feature(q_ref[:, cols(h)].astype(F32)).astype(BF16)
            fq_ref[h] = fq
            scores = (mm(fq, fk_ref[h], 1, 1) * visible_ref[...]).astype(BF16)
            sc_ref[h] = scores
            att_ref[h] = mm(scores, v_ref[:, cols(h)], 1, 0)
        return carry

    lax.fori_loop(0, groups, local_lap, 0)
    loads[3].wait()

    def owner(stage, back):
        kind = 3 if back else 0

        def gather(n, total):
            i = (mine - n) % heads if not back else (mine + n) % heads

            @pl.when(n > 0)
            def _():
                receive(stage, i)

            return total + state_in[stage, i].astype(F32) * weight_ref[kind, i]

        total = lax.fori_loop(0, heads, gather, jnp.zeros((DH, DH), F32))
        total_out[back] = total.astype(BF16)
        copies = []
        for n in range(1, reach + 1):
            target = (z + n) % planes if not back else (z + planes - n) % planes
            copy = pltpu.make_async_remote_copy(
                src_ref=total_out.at[back],
                dst_ref=total_in.at[back, n - 1],
                send_sem=zsend_sem.at[back, n - 1],
                recv_sem=zrecv_sem.at[back, n - 1],
                device_id=plane_peer(target),
                device_id_type=MESH,
            )
            copy.start()
            copies.append(copy)
        carry = jnp.zeros((DH, DH), F32)
        for n in range(1, reach + 1):
            copies[n - 1].wait_recv()
            if not back:
                source = z - n
                inside = source >= 0
                doc = doc_of((source + 1) * (heads * DH) - 1)
                near = doc_of(plane_start - 1)
            else:
                source = z + n
                inside = source < planes
                doc = doc_of(source * (heads * DH))
                near = doc_of(plane_start + heads * DH)
            scale = jnp.where(inside, equal(doc, near), 0.0)
            carry = carry + total_in[back, n - 1].astype(F32) * scale

        def scan(n, run):
            i = n if not back else heads - 1 - n
            state_out[stage + 1, i] = (run * weight_ref[kind + 2, i]).astype(BF16)
            return state_in[stage, i].astype(F32) + run * weight_ref[kind + 1, i]

        lax.fori_loop(0, heads, scan, carry)

        def spread(n, c):
            send(stage + 1, (mine + n) % heads)
            return c

        lax.fori_loop(1, heads, spread, 0)
        to_own(stage + 1)
        return copies

    forward_copies = owner(0, 0)

    def attend(kk):
        h = (mine + heads - kk) % heads
        head_rows = rows_ref[0]
        fq = fq_ref[h]
        att = att_ref[h] + mm(fq, state_in[1, h], 1, 0) * head_rows
        inv = lax.rsqrt(jnp.mean(att * att, axis=-1, keepdims=True) + 1e-05)
        normed = att * inv
        o_ref[:, cols(h)] = normed.astype(BF16)
        grad = g_ref[:, cols(h)].astype(F32)
        ga = ((grad - normed * jnp.mean(grad * normed, axis=-1, keepdims=True)) * inv).astype(BF16)
        ga_ref[h] = ga
        masked = (fq.astype(F32) * head_rows).astype(BF16)
        state_out[2, h] = mm(masked, ga, 0, 0).astype(BF16)

    def attend_lap(it, carry):
        for j in range(UNROLL):
            kk = it * UNROLL + j

            @pl.when(kk > 0)
            def _():
                receive(1, (mine + heads - kk) % heads)

        for j in range(UNROLL):
            attend(it * UNROLL + j)
        for j in range(UNROLL):
            kk = it * UNROLL + j

            @pl.when(kk > 0)
            def _():
                send(2, (mine + heads - kk) % heads)

        return carry

    lax.fori_loop(0, groups, attend_lap, 0)
    to_own(2)
    store_out = pltpu.make_async_copy(o_ref, o_hbm, load_sem.at[4])
    store_out.start()

    def local_back(it, carry):
        for j in range(UNROLL):
            h = it * UNROLL + j
            ga, fq, fk = ga_ref[h], fq_ref[h], fk_ref[h]
            grads = (mm(ga, v_ref[:, cols(h)], 1, 1) * visible_ref[...]).astype(BF16)
            gfq = mm(grads, fk, 1, 0) + mm(ga, state_in[1, h], 1, 1) * rows_ref[0]
            gq_ref[:, cols(h)] = (gfq * slope(q_ref[:, cols(h)].astype(F32))).astype(BF16)
            gfk_ref[h] = mm(grads, fq, 0, 0)
            gfv_ref[h] = mm(sc_ref[h], ga, 0, 0)
        return carry

    lax.fori_loop(0, groups, local_back, 0)
    store_gq = pltpu.make_async_copy(gq_ref, gq_hbm, load_sem.at[5])
    store_gq.start()

    back_copies = owner(2, 1)

    def finish(it, carry):
        for j in range(UNROLL):
            kk = it * UNROLL + j

            @pl.when(kk > 0)
            def _():
                receive(3, (mine + heads - kk) % heads)

        for j in range(UNROLL):
            h = (mine + heads - (it * UNROLL + j)) % heads
            outgoing = state_in[3, h]
            gfk = gfk_ref[h] + mm(v_ref[:, cols(h)], outgoing, 1, 1) * rows_ref[1]
            gk_ref[:, cols(h)] = (gfk * slope(k_ref[:, cols(h)].astype(F32))).astype(BF16)
            gfv = gfv_ref[h] + mm(fk_ref[h], outgoing, 1, 0) * rows_ref[1]
            gv_ref[:, cols(h)] = gfv.astype(BF16)
        return carry

    lax.fori_loop(0, groups, finish, 0)
    store_gk = pltpu.make_async_copy(gk_ref, gk_hbm, load_sem.at[6])
    store_gv = pltpu.make_async_copy(gv_ref, gv_hbm, load_sem.at[7])
    store_gk.start()
    store_gv.start()

    def drain(n, carry):
        p = (mine + n) % heads
        for stage in range(4):
            remote(stage, p, mine, p).wait_send()
        return carry

    lax.fori_loop(1, heads, drain, 0)
    for copy in forward_copies + back_copies:
        copy.wait_send()
    store_out.wait()
    store_gq.wait()
    store_gk.wait()
    store_gv.wait()


def solution(mesh):
    seq_axis, head_axis = mesh.shape["seq"], mesh.shape["head"]

    def local(queries, keys, values, out_grad, doc_lengths):
        rows, width = queries.shape
        heads = width // DH
        plane_seq = heads // head_axis
        planes = seq_axis // plane_seq
        reach = min(planes - 1, -(-DOC_MOST // (heads * DH)))
        cfg = (heads, plane_seq, head_axis, planes, reach)
        flat = [pltpu.VMEM((rows, width), BF16)] * 8
        per_head = [pltpu.VMEM((heads, DH, DH), BF16)] * 4
        wide = [pltpu.VMEM((heads, DH, DH), F32)] * 3
        out = jax.ShapeDtypeStruct((rows, width), BF16)
        hbm = pl.BlockSpec(memory_space=pl.ANY)
        return pl.pallas_call(
            functools.partial(kernel, cfg),
            out_shape=(out,) * 4,
            in_specs=[pl.BlockSpec(memory_space=pltpu.SMEM)] + [hbm] * 4,
            out_specs=(hbm,) * 4,
            scratch_shapes=flat
            + per_head
            + wide
            + [
                pltpu.VMEM((4, heads, DH, DH), BF16),
                pltpu.VMEM((4, heads, DH, DH), BF16),
                pltpu.VMEM((2, DH, DH), BF16),
                pltpu.VMEM((2, reach, DH, DH), BF16),
                pltpu.VMEM((DH, DH), F32),
                pltpu.VMEM((2, DH, DH), F32),
                pltpu.SMEM((6, heads), F32),
                pltpu.SemaphoreType.DMA((4, heads)),
                pltpu.SemaphoreType.DMA((4, heads)),
                pltpu.SemaphoreType.DMA((2, reach)),
                pltpu.SemaphoreType.DMA((2, reach)),
                pltpu.SemaphoreType.DMA((8,)),
            ],
            compiler_params=pltpu.CompilerParams(
                collective_id=0, has_side_effects=True, vmem_limit_bytes=56 << 20
            ),
        )(doc_lengths, queries, keys, values, out_grad)

    return jax.shard_map(
        local,
        mesh=mesh,
        in_specs=(P(("seq", "head"), None),) * 4 + (P(),),
        out_specs=(P(("seq", "head"), None),) * 4,
        check_vma=False,
    )
```

time: 791 us -> 95.4 us (0.12); the launches traced: 780 us -> 93.5 us
  blocking collectives: 264 us -> 0 us
  other arithmetic: 189 us -> 0 us
  local copies, waits for them, and re-layouts: 138 us -> 6.55 us
  Pallas kernels: 0 us -> 86.3 us
  loops' own time: 80.1 us -> 0 us
  starting transfers between devices: 34.7 us -> 0 us
  waiting for transfers between devices: 27.5 us -> 0 us
  matrix products: 26.3 us -> 0 us
  between operations: 19.7 us -> 0.65 us
    unnamed x2 -> x0, blocking collectives: 264 us -> none
    select_n x66 -> x0, other arithmetic: 100 us -> none  [the longest x63 93.2 us: lap(): jnp.where(position < mine, new, old)]
    pallas_call x0 -> x1, Pallas kernels: none -> 86.3 us  [local(): pl.pallas_call(functools.partial(kernel, cfg), out_shape=(out,) * 4, in_s...]
    another operation x2 -> x0, loops' own time: 80.1 us -> none  [the longest x1 42.3 us: prefix_2(): return lax.fori_loop(0, ahead, one, state)]
    dynamic_slice x125 -> x0, local copies, waits for them, and re-layouts: 73.8 us -> none  [the longest x63 37.2 us: lap(): longer = join(so_far, jax.tree.map(lambda part: part[position], pieces))]
    add x63 -> x0, other arithmetic: 72 us -> none  [the longest x62 72 us: linked(): later[0] + (1.0 - later[1]) * earlier[0]]
    all_to_all x8 -> x0, starting transfers between devices: 34.6 us -> none  [the longest x1 5.13 us: local(): lax.all_to_all(keys, 'head', split_axis=1, concat_axis=0, tiled=True)]
    all_to_all x8 -> x0, waiting for transfers between devices: 27.4 us -> none  [the longest x1 12.3 us: local(): lax.all_to_all(keys, 'head', split_axis=1, concat_axis=0, tiled=True)]
  transfers between devices with their start and end apart: 10 -> 0, of which waited for: 4 -> 0; matrix products, arithmetic and copies ran while one was open for 26% -> 0% of each run, Pallas kernels for 0% -> 0%
where the time goes in v1:
time: 95.4 us; the launch traced here: 93.5 us
  Pallas kernels  86.3 us (90%)
  local copies, waits for them, and re-layouts  6.55 us (7%)
    pallas_call x1, Pallas kernels, local(): pl.pallas_call(functools.partial(kernel, cfg), out_shape=(out,) * 4, in_s...  86.3 us
    unnamed x10, local copies, waits for them, and re-layouts  6.55 us

profile of v1, /device:TPU:1, one launch (start us, length us, event | category | flops | bytes accessed | tf_op | source)
XLA Modules:
  0.0 93.5 jit_solution(14751529411491954164)
XLA Ops:
  0.6 86.3 %shard_map.84 = (bf16[128,4096]{1,0:T(8,128)(2,1)}, bf16[128,4096]{1,0:T(8,128)(2,1)}, bf16[128,4096]{1,0:T(8,128)(2,1)}, bf16[128,4096]{1,0:T(8,128)(2,1)}) custom-call(s32[8]{0:T(128)} %len_ref.1, bf16[128,4096]{1,0:T(8,128)(2,1)} %q_hbm.1, bf16[128,4096]{1,0:T(8,128)(2,1)} %k_hbm.1, bf16[128,4096]{1,0:T(8,128)(2,1)} %v_hbm.1, bf16[128,4096]{1,0:T(8,128)(2,1)} %g_hbm.1), custom_call_target="tpu_custom_call" | custom-call | tf_op jit(solution)/shard_map/pallas_call | solution.py:376
  86.9 0.0 copy-start.2
  86.9 2.4 %copy.13 = bf16[128,4096]{1,0:T(8,128)(2,1)} copy(bf16[128,4096]{1,0:T(8,128)(2,1)} %get-tuple-element.8) | data formatting | bytes 2097152
  89.3 0.0 copy-done.2
  89.3 0.0 copy-start.1
  89.3 1.0 %copy.14 = bf16[128,4096]{1,0:T(8,128)(2,1)} copy(bf16[128,4096]{1,0:T(8,128)(2,1)S(1)} %copy-done.2) | data formatting | bytes 2097152
  90.3 0.6 copy-done.1
  90.9 0.0 copy-start
  90.9 1.0 %copy.15 = bf16[128,4096]{1,0:T(8,128)(2,1)} copy(bf16[128,4096]{1,0:T(8,128)(2,1)S(1)} %copy-done.1) | data formatting | bytes 2097152
  91.9 0.6 copy-done
  92.5 1.0 %copy.16 = bf16[128,4096]{1,0:T(8,128)(2,1)} copy(bf16[128,4096]{1,0:T(8,128)(2,1)S(1)} %copy-done) | data formatting | bytes 2097152
Async XLA Ops:
  86.9 2.4 %copy-start.2 = (bf16[128,4096]{1,0:T(8,128)(2,1)S(1)}, bf16[128,4096]{1,0:T(8,128)(2,1)}, u32[]{:S(2)}) copy-start(bf16[128,4096]{1,0:T(8,128)(2,1)} %get-tuple-element.9) | copy-start | bytes 3145732
  89.3 1.6 %copy-start.1 = (bf16[128,4096]{1,0:T(8,128)(2,1)S(1)}, bf16[128,4096]{1,0:T(8,128)(2,1)}, u32[]{:S(2)}) copy-start(bf16[128,4096]{1,0:T(8,128)(2,1)} %get-tuple-element.10) | copy-start | bytes 3145732
  90.9 1.6 %copy-start = (bf16[128,4096]{1,0:T(8,128)(2,1)S(1)}, bf16[128,4096]{1,0:T(8,128)(2,1)}, u32[]{:S(2)}) copy-start(bf16[128,4096]{1,0:T(8,128)(2,1)} %get-tuple-element.11) | copy-start | bytes 3145732

commit v2 on v1

v2 whole, which is shorter than its diff:
```python
import functools

import jax
import jax.numpy as jnp
from jax import lax
from jax.experimental import pallas as pl
from jax.experimental.pallas import tpu as pltpu
from jax.sharding import PartitionSpec as P

DH = 128
DOC_MOST = 16384
UNROLL = 4
GROUPS = 4
MESH = pl.DeviceIdType.MESH
F32 = jnp.float32
BF16 = jnp.bfloat16


def mm(a, b, ca, cb):
    return lax.dot_general(a, b, (((ca,), (cb,)), ((), ())), preferred_element_type=F32)


def feature(x):
    return jnp.where(x > 0, x + 1.0, jnp.exp(jnp.minimum(x, 0.0)))


def slope(x):
    return jnp.where(x > 0, 1.0, jnp.exp(jnp.minimum(x, 0.0)))


def kernel(
    cfg,
    len_ref,
    q_hbm,
    k_hbm,
    v_hbm,
    g_hbm,
    o_hbm,
    gq_hbm,
    gk_hbm,
    gv_hbm,
    q_ref,
    k_ref,
    v_ref,
    g_ref,
    o_ref,
    gq_ref,
    gk_ref,
    gv_ref,
    fq_ref,
    fk_ref,
    sc_ref,
    ga_ref,
    att_ref,
    gfk_ref,
    gfv_ref,
    state_out,
    state_in,
    prefix_out,
    prefix_in,
    total_out,
    total_in,
    visible_ref,
    rows_ref,
    weight_ref,
    send_sem,
    state_sem,
    prefix_sem,
    zsend_sem,
    zrecv_sem,
    load_sem,
):
    heads, plane_seq, head_axis, planes, reach = cfg
    per_group = heads // GROUPS
    laps = per_group // UNROLL
    slab = DH // GROUPS
    seq = lax.axis_index("seq")
    place = lax.axis_index("head")
    z = seq // plane_seq
    mine = (seq % plane_seq) * head_axis + place
    block = z * heads + mine

    def peer(p):
        return (z * plane_seq + p // head_axis, p % head_axis)

    def plane_peer(other):
        return (other * plane_seq + seq % plane_seq, place)

    def cols(h):
        return pl.ds(pl.multiple_of(h * DH, DH), DH)

    loads = [
        pltpu.make_async_copy(src, dst, load_sem.at[n])
        for n, (src, dst) in enumerate(
            ((k_hbm, k_ref), (v_hbm, v_ref), (q_hbm, q_ref), (g_hbm, g_ref))
        )
    ]
    for load in loads:
        load.start()

    barrier = pltpu.get_barrier_semaphore()

    def greet(n, carry):
        pl.semaphore_signal(
            barrier, inc=1, device_id=peer((mine + n) % heads), device_id_type=MESH
        )
        return carry

    lax.fori_loop(1, heads, greet, 0)
    for n in range(1, planes):
        pl.semaphore_signal(
            barrier, inc=1, device_id=plane_peer((z + n) % planes), device_id_type=MESH
        )

    ends = []
    end = jnp.int32(0)
    for n in range(len_ref.shape[0]):
        end = end + len_ref[n]
        ends.append(end)

    def doc_of(where):
        return sum([(where >= e).astype(jnp.int32) for e in ends])

    def equal(a, b):
        return jnp.where(a == b, 1.0, 0.0).astype(F32)

    start = block * DH
    row_doc = doc_of(start + lax.broadcasted_iota(jnp.int32, (DH, DH), 0))
    col_doc = doc_of(start + lax.broadcasted_iota(jnp.int32, (DH, DH), 1))
    causal = lax.broadcasted_iota(jnp.int32, (DH, DH), 0) >= lax.broadcasted_iota(
        jnp.int32, (DH, DH), 1
    )
    visible_ref[...] = jnp.where(causal & (row_doc == col_doc), 1.0, 0.0).astype(F32)
    rows_ref[0] = jnp.where(row_doc == doc_of(start), 1.0, 0.0).astype(F32)
    rows_ref[1] = jnp.where(row_doc == doc_of(start + DH - 1), 1.0, 0.0).astype(F32)

    plane_start = z * (heads * DH)
    plane_first = doc_of(plane_start)
    plane_last = doc_of(plane_start + heads * DH - 1)

    def weigh(i, carry):
        begin = plane_start + i * DH
        before, first = doc_of(begin - 1), doc_of(begin)
        last, after = doc_of(begin + DH - 1), doc_of(begin + DH)
        weight_ref[0, i] = equal(last, plane_last)
        weight_ref[1, i] = equal(last, before)
        weight_ref[2, i] = equal(first, before)
        weight_ref[3, i] = equal(first, plane_first)
        weight_ref[4, i] = equal(first, after)
        weight_ref[5, i] = equal(last, after)
        return carry

    lax.fori_loop(0, heads, weigh, 0)

    def owned(g):
        return g * per_group + mine // GROUPS

    def slab_rows(s):
        return pl.ds(pl.multiple_of(s * slab, slab), slab)

    def state_copy(way, g, p):
        source = state_out.at[way, g * per_group + p // GROUPS, slab_rows(p % GROUPS)]
        return source, state_in.at[way, g, mine], state_sem.at[way, g]

    def prefix_copy(way, g, p):
        target = prefix_in.at[way, owned(g), slab_rows(mine % GROUPS)]
        return prefix_out.at[way, g, p], target, prefix_sem.at[way, owned(g)]

    def remote(refs, sem, p):
        return pltpu.make_async_remote_copy(
            src_ref=refs[0],
            dst_ref=refs[1],
            send_sem=sem,
            recv_sem=refs[2],
            device_id=peer(p),
            device_id_type=MESH,
        )

    def dispatch(refs, sem, p):
        own = p == mine

        @pl.when(own)
        def _():
            pltpu.make_async_copy(*refs).start()

        @pl.when(jnp.logical_not(own))
        def _():
            remote(refs, sem, p).start()

    def send_states(way, g, a):
        for s in range(GROUPS):
            p = a * GROUPS + (mine + s) % GROUPS
            dispatch(state_copy(way, g, p), send_sem.at[way, 0], p)

    def ahead(it, j):
        g, lap = it // laps, it % laps
        return g, (mine // GROUPS + lap * UNROLL + j) % per_group

    def forward_lap(it, carry):
        @pl.when(it < GROUPS * laps)
        def _():
            for j in range(UNROLL):
                g, a = ahead(it, j)
                h = g * per_group + a
                fk = feature(k_ref[:, cols(h)].astype(F32))
                fk_ref[h] = fk.astype(BF16)
                masked = (fk * rows_ref[1]).astype(BF16)
                state_out[0, h] = mm(masked, v_ref[:, cols(h)], 0, 0).astype(BF16)

        @pl.when(it == 1)
        def _():
            pl.semaphore_wait(barrier, heads - 1 + planes - 1)

        @pl.when(it > 0)
        def _():
            for j in range(UNROLL):
                g, a = ahead(it - 1, j)
                send_states(0, g, a)

        return carry

    def local_forward(g):
        def lap(it, carry):
            for j in range(UNROLL):
                h = g * per_group + it * UNROLL + j
                fq = feature(q_ref[:, cols(h)].astype(F32)).astype(BF16)
                fq_ref[h] = fq
                scores = (mm(fq, fk_ref[h], 1, 1) * visible_ref[...]).astype(BF16)
                sc_ref[h] = scores
                att_ref[h] = mm(scores, v_ref[:, cols(h)], 1, 0)
            return carry

        lax.fori_loop(0, laps, lap, 0)

    def total_copy(way, g, n):
        target = (z + n) % planes if way == 0 else (z + planes - n) % planes
        return pltpu.make_async_remote_copy(
            src_ref=total_out.at[way, g],
            dst_ref=total_in.at[way, g, n - 1],
            send_sem=zsend_sem.at[way],
            recv_sem=zrecv_sem.at[way, g, n - 1],
            device_id=plane_peer(target),
            device_id_type=MESH,
        )

    def sum_up(way, g):
        pltpu.make_async_copy(state_in.at[way, g], state_in.at[way, g], state_sem.at[way, g]).wait()

        def add(n, total):
            for j in range(4):
                i = n * 4 + j
                total = total + state_in[way, g, i].astype(F32) * weight_ref[3 * way, i]
            return total

        total = lax.fori_loop(0, heads // 4, add, jnp.zeros((slab, DH), F32))
        total_out[way, g] = total.astype(BF16)
        for n in range(1, reach + 1):
            total_copy(way, g, n).start()

    def scan(way, g):
        run = jnp.zeros((slab, DH), F32)
        for n in range(1, reach + 1):
            total_copy(way, g, n).wait_recv()
            if way == 0:
                source = z - n
                inside = source >= 0
                doc = doc_of((source + 1) * (heads * DH) - 1)
                near = doc_of(plane_start - 1)
            else:
                source = z + n
                inside = source < planes
                doc = doc_of(source * (heads * DH))
                near = doc_of(plane_start + heads * DH)
            scale = jnp.where(inside, equal(doc, near), 0.0)
            run = run + total_in[way, g, n - 1].astype(F32) * scale

        def step(n, run):
            for j in range(4):
                i = n * 4 + j
                i = i if way == 0 else heads - 1 - i
                prefix_out[way, g, i] = (run * weight_ref[3 * way + 2, i]).astype(BF16)
                run = state_in[way, g, i].astype(F32) + run * weight_ref[3 * way + 1, i]
            return run

        lax.fori_loop(0, heads // 4, step, run)

        def spread(n, carry):
            p = (mine + n) % heads
            dispatch(prefix_copy(way, g, p), send_sem.at[way, 1], p)
            return carry

        lax.fori_loop(0, heads, spread, 0)

    def arrive(way, h):
        pltpu.make_async_copy(prefix_in.at[way, h], prefix_in.at[way, h], prefix_sem.at[way, h]).wait()

    def behind(it, j):
        g, lap = it // laps, it % laps
        return g, (mine // GROUPS + per_group - lap * UNROLL - j) % per_group

    def attend_lap(it, carry):
        @pl.when(it < GROUPS * laps)
        def _():
            spots = [behind(it, j) for j in range(UNROLL)]
            for g, a in spots:
                arrive(0, g * per_group + a)
            for g, a in spots:
                h = g * per_group + a
                head_rows = rows_ref[0]
                fq = fq_ref[h]
                att = att_ref[h] + mm(fq, prefix_in[0, h], 1, 0) * head_rows
                inv = lax.rsqrt(jnp.mean(att * att, axis=-1, keepdims=True) + 1e-05)
                normed = att * inv
                o_ref[:, cols(h)] = normed.astype(BF16)
                grad = g_ref[:, cols(h)].astype(F32)
                mean = jnp.mean(grad * normed, axis=-1, keepdims=True)
                ga = ((grad - normed * mean) * inv).astype(BF16)
                ga_ref[h] = ga
                masked = (fq.astype(F32) * head_rows).astype(BF16)
                state_out[1, h] = mm(masked, ga, 0, 0).astype(BF16)

        @pl.when(it > 0)
        def _():
            for j in range(UNROLL):
                g, a = behind(it - 1, j)
                send_states(1, g, a)

        return carry

    def local_back(g):
        def lap(it, carry):
            for j in range(UNROLL):
                h = g * per_group + it * UNROLL + j
                ga, fq, fk = ga_ref[h], fq_ref[h], fk_ref[h]
                grads = (mm(ga, v_ref[:, cols(h)], 1, 1) * visible_ref[...]).astype(BF16)
                gfq = mm(grads, fk, 1, 0) + mm(ga, prefix_in[0, h], 1, 1) * rows_ref[0]
                gq_ref[:, cols(h)] = (gfq * slope(q_ref[:, cols(h)].astype(F32))).astype(BF16)
                gfk_ref[h] = mm(grads, fq, 0, 0)
                gfv_ref[h] = mm(sc_ref[h], ga, 0, 0)
            return carry

        lax.fori_loop(0, laps, lap, 0)

    def finish(it, carry):
        spots = [behind(it, j) for j in range(UNROLL)]
        for g, a in spots:
            arrive(1, g * per_group + a)
        for g, a in spots:
            h = g * per_group + a
            outgoing = prefix_in[1, h]
            gfk = gfk_ref[h] + mm(v_ref[:, cols(h)], outgoing, 1, 1) * rows_ref[1]
            gk_ref[:, cols(h)] = (gfk * slope(k_ref[:, cols(h)].astype(F32))).astype(BF16)
            gfv = gfv_ref[h] + mm(fk_ref[h], outgoing, 1, 0) * rows_ref[1]
            gv_ref[:, cols(h)] = gfv.astype(BF16)
        return carry

    def each_group(way, local, g, carry):
        local(g)
        sum_up(way, g)
        return carry

    def each_scan(way, g, carry):
        scan(way, g)
        return carry

    stores = [
        pltpu.make_async_copy(src, dst, load_sem.at[4 + n])
        for n, (src, dst) in enumerate(
            ((o_ref, o_hbm), (gq_ref, gq_hbm), (gk_ref, gk_hbm), (gv_ref, gv_hbm))
        )
    ]
    loads[0].wait()
    loads[1].wait()
    lax.fori_loop(0, GROUPS * laps + 1, forward_lap, 0)
    loads[2].wait()
    lax.fori_loop(0, GROUPS, functools.partial(each_group, 0, local_forward), 0)
    lax.fori_loop(0, GROUPS, functools.partial(each_scan, 0), 0)
    loads[3].wait()
    lax.fori_loop(0, GROUPS * laps + 1, attend_lap, 0)
    stores[0].start()
    lax.fori_loop(0, GROUPS, functools.partial(each_group, 1, local_back), 0)
    stores[1].start()
    lax.fori_loop(0, GROUPS, functools.partial(each_scan, 1), 0)
    lax.fori_loop(0, GROUPS * laps, finish, 0)
    stores[2].start()
    stores[3].start()

    for way in range(2):
        for n in range(2):
            sent = state_out.at[way, pl.ds(0, heads - 1)]
            pltpu.make_async_copy(sent, sent, send_sem.at[way, n]).wait()
        for n in range(1, reach + 1):
            pltpu.make_async_copy(total_out.at[way], total_out.at[way], zsend_sem.at[way]).wait()
    for store in stores:
        store.wait()


def solution(mesh):
    seq_axis, head_axis = mesh.shape["seq"], mesh.shape["head"]

    def local(queries, keys, values, out_grad, doc_lengths):
        rows, width = queries.shape
        heads = width // DH
        plane_seq = heads // head_axis
        planes = seq_axis // plane_seq
        reach = min(planes - 1, -(-DOC_MOST // (heads * DH)))
        cfg = (heads, plane_seq, head_axis, planes, reach)
        flat = [pltpu.VMEM((rows, width), BF16)] * 8
        per_head = [pltpu.VMEM((heads, DH, DH), BF16)] * 4
        wide = [pltpu.VMEM((heads, DH, DH), F32)] * 3
        out = jax.ShapeDtypeStruct((rows, width), BF16)
        hbm = pl.BlockSpec(memory_space=pl.ANY)
        return pl.pallas_call(
            functools.partial(kernel, cfg),
            out_shape=(out,) * 4,
            in_specs=[pl.BlockSpec(memory_space=pltpu.SMEM)] + [hbm] * 4,
            out_specs=(hbm,) * 4,
            scratch_shapes=flat
            + per_head
            + wide
            + [
                pltpu.VMEM((2, heads, DH, DH), BF16),
                pltpu.VMEM((2, GROUPS, heads, DH // GROUPS, DH), BF16),
                pltpu.VMEM((2, GROUPS, heads, DH // GROUPS, DH), BF16),
                pltpu.VMEM((2, heads, DH, DH), BF16),
                pltpu.VMEM((2, GROUPS, DH // GROUPS, DH), BF16),
                pltpu.VMEM((2, GROUPS, reach, DH // GROUPS, DH), BF16),
                pltpu.VMEM((DH, DH), F32),
                pltpu.VMEM((2, DH, DH), F32),
                pltpu.SMEM((6, heads), F32),
                pltpu.SemaphoreType.DMA((2, 2)),
                pltpu.SemaphoreType.DMA((2, GROUPS)),
                pltpu.SemaphoreType.DMA((2, heads)),
                pltpu.SemaphoreType.DMA((2,)),
                pltpu.SemaphoreType.DMA((2, GROUPS, reach)),
                pltpu.SemaphoreType.DMA((8,)),
            ],
            compiler_params=pltpu.CompilerParams(
                collective_id=0, has_side_effects=True, vmem_limit_bytes=56 << 20
            ),
        )(doc_lengths, queries, keys, values, out_grad)

    return jax.shard_map(
        local,
        mesh=mesh,
        in_specs=(P(("seq", "head"), None),) * 4 + (P(),),
        out_specs=(P(("seq", "head"), None),) * 4,
        check_vma=False,
    )
```

time: 95.4 us -> 78.5 us (0.82); the launches traced: 93.5 us -> 78.3 us
  Pallas kernels: 86.3 us -> 71.1 us
    pallas_call x1, Pallas kernels: 86.3 us -> 71.1 us  [local(): pl.pallas_call(functools.partial(kernel, cfg), out_shape=(out,) * 4, in_s...]
where the time goes in v2:
time: 78.5 us; the launch traced here: 78.3 us
  Pallas kernels  71.1 us (91%)
  local copies, waits for them, and re-layouts  6.55 us (8%)
    pallas_call x1, Pallas kernels, local(): pl.pallas_call(functools.partial(kernel, cfg), out_shape=(out,) * 4, in_s...  71.1 us
    unnamed x10, local copies, waits for them, and re-layouts  6.55 us

profile of v2, /device:TPU:1, one launch (start us, length us, event | category | flops | bytes accessed | tf_op | source)
XLA Modules:
  0.0 78.3 jit_solution(15395218818677229450)
XLA Ops:
  0.6 71.1 %shard_map.84 = (bf16[128,4096]{1,0:T(8,128)(2,1)}, bf16[128,4096]{1,0:T(8,128)(2,1)}, bf16[128,4096]{1,0:T(8,128)(2,1)}, bf16[128,4096]{1,0:T(8,128)(2,1)}) custom-call(s32[8]{0:T(128)} %len_ref.1, bf16[128,4096]{1,0:T(8,128)(2,1)} %q_hbm.1, bf16[128,4096]{1,0:T(8,128)(2,1)} %k_hbm.1, bf16[128,4096]{1,0:T(8,128)(2,1)} %v_hbm.1, bf16[128,4096]{1,0:T(8,128)(2,1)} %g_hbm.1), custom_call_target="tpu_custom_call" | custom-call | tf_op jit(solution)/shard_map/pallas_call | solution.py:413
  71.7 0.0 copy-start.2
  71.7 2.4 %copy.13 = bf16[128,4096]{1,0:T(8,128)(2,1)} copy(bf16[128,4096]{1,0:T(8,128)(2,1)} %get-tuple-element.8) | data formatting | bytes 2097152
  74.1 0.0 copy-done.2
  74.1 0.0 copy-start.1
  74.1 1.0 %copy.14 = bf16[128,4096]{1,0:T(8,128)(2,1)} copy(bf16[128,4096]{1,0:T(8,128)(2,1)S(1)} %copy-done.2) | data formatting | bytes 2097152
  75.1 0.6 copy-done.1
  75.7 0.0 copy-start
  75.7 1.0 %copy.15 = bf16[128,4096]{1,0:T(8,128)(2,1)} copy(bf16[128,4096]{1,0:T(8,128)(2,1)S(1)} %copy-done.1) | data formatting | bytes 2097152
  76.7 0.6 copy-done
  77.3 1.0 %copy.16 = bf16[128,4096]{1,0:T(8,128)(2,1)} copy(bf16[128,4096]{1,0:T(8,128)(2,1)S(1)} %copy-done) | data formatting | bytes 2097152
Async XLA Ops:
  71.7 2.4 %copy-start.2 = (bf16[128,4096]{1,0:T(8,128)(2,1)S(1)}, bf16[128,4096]{1,0:T(8,128)(2,1)}, u32[]{:S(2)}) copy-start(bf16[128,4096]{1,0:T(8,128)(2,1)} %get-tuple-element.9) | copy-start | bytes 3145732
  74.1 1.6 %copy-start.1 = (bf16[128,4096]{1,0:T(8,128)(2,1)S(1)}, bf16[128,4096]{1,0:T(8,128)(2,1)}, u32[]{:S(2)}) copy-start(bf16[128,4096]{1,0:T(8,128)(2,1)} %get-tuple-element.10) | copy-start | bytes 3145732
  75.7 1.6 %copy-start = (bf16[128,4096]{1,0:T(8,128)(2,1)S(1)}, bf16[128,4096]{1,0:T(8,128)(2,1)}, u32[]{:S(2)}) copy-start(bf16[128,4096]{1,0:T(8,128)(2,1)} %get-tuple-element.11) | copy-start | bytes 3145732

commit v3 on v2

--- a/solution.py
+++ b/solution.py
@@ -11,6 +11,8 @@
 DOC_MOST = 16384
 UNROLL = 4
 GROUPS = 4
+SCHEDULE = "L0T0L1T1P0L2T2P1L3T3P2P3A0A1A2A3M0M1U0U1M2Q0U2Q1U3M3Q2Q3F0F1F2F3"
+KERNEL_VMEM_KIB = 60928
 MESH = pl.DeviceIdType.MESH
 F32 = jnp.float32
 BF16 = jnp.bfloat16
@@ -35,18 +37,14 @@
     k_hbm,
     v_hbm,
     g_hbm,
-    o_hbm,
-    gq_hbm,
-    gk_hbm,
-    gv_hbm,
+    o_ref,
+    gq_ref,
+    gk_ref,
+    gv_ref,
     q_ref,
     k_ref,
     v_ref,
     g_ref,
-    o_ref,
-    gq_ref,
-    gk_ref,
-    gv_ref,
     fq_ref,
     fk_ref,
     sc_ref,
@@ -294,17 +292,16 @@
     def arrive(way, h):
         pltpu.make_async_copy(prefix_in.at[way, h], prefix_in.at[way, h], prefix_sem.at[way, h]).wait()
 
-    def behind(it, j):
-        g, lap = it // laps, it % laps
-        return g, (mine // GROUPS + per_group - lap * UNROLL - j) % per_group
-
-    def attend_lap(it, carry):
-        @pl.when(it < GROUPS * laps)
+    def behind(lap, j):
+        return (mine // GROUPS + per_group - lap * UNROLL - j) % per_group
+
+    def attend_lap(g, it, carry):
+        @pl.when(it < laps)
         def _():
             spots = [behind(it, j) for j in range(UNROLL)]
-            for g, a in spots:
+            for a in spots:
                 arrive(0, g * per_group + a)
-            for g, a in spots:
+            for a in spots:
                 h = g * per_group + a
                 head_rows = rows_ref[0]
                 fq = fq_ref[h]
@@ -322,8 +319,7 @@
         @pl.when(it > 0)
         def _():
             for j in range(UNROLL):
-                g, a = behind(it - 1, j)
-                send_states(1, g, a)
+                send_states(1, g, behind(it - 1, j))
 
         return carry
 
@@ -341,11 +337,11 @@
 
         lax.fori_loop(0, laps, lap, 0)
 
-    def finish(it, carry):
+    def finish_lap(g, it, carry):
         spots = [behind(it, j) for j in range(UNROLL)]
-        for g, a in spots:
+        for a in spots:
             arrive(1, g * per_group + a)
-        for g, a in spots:
+        for a in spots:
             h = g * per_group + a
             outgoing = prefix_in[1, h]
             gfk = gfk_ref[h] + mm(v_ref[:, cols(h)], outgoing, 1, 1) * rows_ref[1]
@@ -354,45 +350,44 @@
             gv_ref[:, cols(h)] = gfv.astype(BF16)
         return carry
 
-    def each_group(way, local, g, carry):
-        local(g)
-        sum_up(way, g)
-        return carry
-
-    def each_scan(way, g, carry):
-        scan(way, g)
-        return carry
-
-    stores = [
-        pltpu.make_async_copy(src, dst, load_sem.at[4 + n])
-        for n, (src, dst) in enumerate(
-            ((o_ref, o_hbm), (gq_ref, gq_hbm), (gk_ref, gk_hbm), (gv_ref, gv_hbm))
-        )
-    ]
+    def attend(g):
+        lax.fori_loop(0, laps + 1, functools.partial(attend_lap, g), 0)
+
+    def finish(g):
+        lax.fori_loop(0, laps, functools.partial(finish_lap, g), 0)
+
     loads[0].wait()
     loads[1].wait()
     lax.fori_loop(0, GROUPS * laps + 1, forward_lap, 0)
     loads[2].wait()
-    lax.fori_loop(0, GROUPS, functools.partial(each_group, 0, local_forward), 0)
-    lax.fori_loop(0, GROUPS, functools.partial(each_scan, 0), 0)
     loads[3].wait()
-    lax.fori_loop(0, GROUPS * laps + 1, attend_lap, 0)
-    stores[0].start()
-    lax.fori_loop(0, GROUPS, functools.partial(each_group, 1, local_back), 0)
-    stores[1].start()
-    lax.fori_loop(0, GROUPS, functools.partial(each_scan, 1), 0)
-    lax.fori_loop(0, GROUPS * laps, finish, 0)
-    stores[2].start()
-    stores[3].start()
-
+    steps = {
+        "L": local_forward,
+        "T": functools.partial(sum_up, 0),
+        "P": functools.partial(scan, 0),
+        "A": attend,
+        "M": local_back,
+        "U": functools.partial(sum_up, 1),
+        "Q": functools.partial(scan, 1),
+        "F": finish,
+    }
+    for n in range(0, len(SCHEDULE), 2):
+        steps[SCHEDULE[n]](int(SCHEDULE[n + 1]))
     for way in range(2):
         for n in range(2):
             sent = state_out.at[way, pl.ds(0, heads - 1)]
             pltpu.make_async_copy(sent, sent, send_sem.at[way, n]).wait()
         for n in range(1, reach + 1):
             pltpu.make_async_copy(total_out.at[way], total_out.at[way], zsend_sem.at[way]).wait()
-    for store in stores:
-        store.wait()
+
+
+def write_out(*refs):
+    sources, targets, sem = refs[:4], refs[4:8], refs[8]
+    copies = [pltpu.make_async_copy(sources[n], targets[n], sem.at[n]) for n in range(4)]
+    for copy in copies:
+        copy.start()
+    for copy in copies:
+        copy.wait()
 
 
 def solution(mesh):
@@ -405,16 +400,16 @@
         planes = seq_axis // plane_seq
         reach = min(planes - 1, -(-DOC_MOST // (heads * DH)))
         cfg = (heads, plane_seq, head_axis, planes, reach)
-        flat = [pltpu.VMEM((rows, width), BF16)] * 8
+        flat = [pltpu.VMEM((rows, width), BF16)] * 4
         per_head = [pltpu.VMEM((heads, DH, DH), BF16)] * 4
         wide = [pltpu.VMEM((heads, DH, DH), F32)] * 3
         out = jax.ShapeDtypeStruct((rows, width), BF16)
         hbm = pl.BlockSpec(memory_space=pl.ANY)
-        return pl.pallas_call(
+        parts = pl.pallas_call(
             functools.partial(kernel, cfg),
-            out_shape=(out,) * 4,
+            out_shape=(pltpu.VMEM((rows, width), BF16),) * 4,
             in_specs=[pl.BlockSpec(memory_space=pltpu.SMEM)] + [hbm] * 4,
-            out_specs=(hbm,) * 4,
+            out_specs=(pl.BlockSpec(memory_space=pltpu.VMEM),) * 4,
             scratch_shapes=flat
             + per_head
             + wide
@@ -433,12 +428,20 @@
                 pltpu.SemaphoreType.DMA((2, heads)),
                 pltpu.SemaphoreType.DMA((2,)),
                 pltpu.SemaphoreType.DMA((2, GROUPS, reach)),
-                pltpu.SemaphoreType.DMA((8,)),
+                pltpu.SemaphoreType.DMA((4,)),
             ],
             compiler_params=pltpu.CompilerParams(
-                collective_id=0, has_side_effects=True, vmem_limit_bytes=56 << 20
+                collective_id=0, has_side_effects=True, vmem_limit_bytes=KERNEL_VMEM_KIB << 10
             ),
         )(doc_lengths, queries, keys, values, out_grad)
+        return pl.pallas_call(
+            write_out,
+            out_shape=(out,) * 4,
+            in_specs=[pl.BlockSpec(memory_space=pltpu.VMEM)] * 4,
+            out_specs=(hbm,) * 4,
+            scratch_shapes=[pltpu.SemaphoreType.DMA((4,))],
+            compiler_params=pltpu.CompilerParams(vmem_limit_bytes=16 << 20),
+        )(*parts)
 
     return jax.shard_map(
         local,

time: 78.5 us -> 70.3 us (0.90)
  local copies, waits for them, and re-layouts: 6.55 us -> 0 us
  Pallas kernels: 71.1 us -> 69.4 us
    unnamed x10 -> x0, local copies, waits for them, and re-layouts: 6.55 us -> none
    pallas_call x1 -> x2, Pallas kernels: 71.1 us -> 69.4 us  [the longest x1 67.4 us: local(): pl.pallas_call(functools.partial(kernel, cfg), out_shape=(pltpu.VMEM((row...]
where the time goes in v3:
time: 70.3 us; the launch traced here: 70.1 us
  Pallas kernels  69.4 us (99%)
    pallas_call x1, Pallas kernels, local(): pl.pallas_call(functools.partial(kernel, cfg), out_shape=(pltpu.VMEM((row...  67.4 us
    pallas_call x1, Pallas kernels, local(): pl.pallas_call(write_out, out_shape=(out,) * 4, in_specs=[pl.BlockSpec(me...  2.04 us

profile of v3, /device:TPU:1, one launch (start us, length us, event | category | flops | bytes accessed | tf_op | source)
XLA Modules:
  0.0 70.1 jit_solution(8240065194929439927)
XLA Ops:
  0.6 67.4 %shard_map.84 = (bf16[128,4096]{1,0:T(8,128)(2,1)S(1)}, bf16[128,4096]{1,0:T(8,128)(2,1)S(1)}, bf16[128,4096]{1,0:T(8,128)(2,1)S(1)}, bf16[128,4096]{1,0:T(8,128)(2,1)S(1)}) custom-call(s32[8]{0:T(128)} %len_ref.1, bf16[128,4096]{1,0:T(8,128)(2,1)} %q_hbm.1, bf16[128,4096]{1,0:T(8,128)(2,1)} %k_hbm.1, bf16[128,4096]{1,0:T(8,128)(2,1)} %v_hbm.1, ...), custom_call_target="tpu_custom_call" | custom-call | tf_op jit(solution)/shard_map/pallas_call | solution.py:408
  68.0 2.0 %shard_map.85 = (bf16[128,4096]{1,0:T(8,128)(2,1)}, bf16[128,4096]{1,0:T(8,128)(2,1)}, bf16[128,4096]{1,0:T(8,128)(2,1)}, bf16[128,4096]{1,0:T(8,128)(2,1)}) custom-call(bf16[128,4096]{1,0:T(8,128)(2,1)S(1)} %get-tuple-element.8.refs_0_, bf16[128,4096]{1,0:T(8,128)(2,1)S(1)} %get-tuple-element.9.refs_1_, bf16[128,4096]{1,0:T(8,128)(2,1)S(1)} %get-tuple-element.10.refs_2_, ...), custom_call_target="tpu_custom_call" | custom-call | tf_op jit(solution)/shard_map/pallas_call | solution.py:437

commit v4 on v3

v4 whole, which is shorter than its diff:
```python
import functools

import jax
import jax.numpy as jnp
from jax import lax
from jax.experimental import pallas as pl
from jax.experimental.pallas import tpu as pltpu
from jax.sharding import PartitionSpec as P

DH = 128
DOC_MOST = 16384
UNROLL = 8
GROUPS = 4
WRITES = 1
SPREAD = 32
SCHEDULE = "L0T0L1T1P0L2T2P1L3T3P2P3A0A1A2A3U0M0U1M1Q0U2M2Q1U3M3Q2Q3F0F1F2F3"
KERNEL_VMEM_KIB = 60928
MESH = pl.DeviceIdType.MESH
F32 = jnp.float32
BF16 = jnp.bfloat16


def mm(a, b, ca, cb):
    return lax.dot_general(a, b, (((ca,), (cb,)), ((), ())), preferred_element_type=F32)


def over(a, n):
    return lax.shift_right_logical(a, n.bit_length() - 1)


def modulo(a, n):
    return lax.bitwise_and(a, n - 1)


def feature(x):
    return jnp.where(x > 0, x + 1.0, jnp.exp(jnp.minimum(x, 0.0)))


def slope(x):
    return jnp.where(x > 0, 1.0, jnp.exp(jnp.minimum(x, 0.0)))


def kernel(
    cfg,
    len_ref,
    q_hbm,
    k_hbm,
    v_hbm,
    g_hbm,
    o_ref,
    gq_ref,
    gk_ref,
    gv_ref,
    q_ref,
    k_ref,
    v_ref,
    g_ref,
    fq_ref,
    fk_ref,
    sc_ref,
    ga_ref,
    att_ref,
    gfk_ref,
    gfv_ref,
    state_out,
    state_in,
    prefix_out,
    prefix_in,
    total_out,
    total_in,
    visible_ref,
    rows_ref,
    weight_ref,
    zweight_ref,
    send_sem,
    state_sem,
    prefix_sem,
    zsend_sem,
    zrecv_sem,
    load_sem,
):
    heads, plane_seq, head_axis, planes, reach = cfg
    per_group = heads // GROUPS
    laps = per_group // UNROLL
    slab = DH // GROUPS
    seq = lax.axis_index("seq")
    place = lax.axis_index("head")
    z = over(seq, plane_seq)
    mine = modulo(seq, plane_seq) * head_axis + place
    my_head, my_slab = over(mine, GROUPS), modulo(mine, GROUPS)
    block = z * heads + mine

    def peer(p):
        return (z * plane_seq + over(p, head_axis), modulo(p, head_axis))

    def plane_peer(other):
        return (other * plane_seq + modulo(seq, plane_seq), place)

    def cols(h):
        return pl.ds(pl.multiple_of(h * DH, DH), DH)

    part = per_group * DH
    first_loads = []
    for g in range(GROUPS):
        chunk = pl.ds(g * part, part)
        first_loads.append(
            [
                pltpu.make_async_copy(src.at[:, chunk], dst.at[:, chunk], load_sem.at[2 + 2 * g + n])
                for n, (src, dst) in enumerate(((k_hbm, k_ref), (v_hbm, v_ref)))
            ]
        )
    late_loads = [
        pltpu.make_async_copy(q_hbm, q_ref, load_sem.at[0]),
        pltpu.make_async_copy(g_hbm, g_ref, load_sem.at[1]),
    ]
    for pair in first_loads:
        for load in pair:
            load.start()

    barrier = pltpu.get_barrier_semaphore()

    def greet(n, carry):
        pl.semaphore_signal(
            barrier, inc=1, device_id=peer(modulo(mine + n, heads)), device_id_type=MESH
        )
        return carry

    lax.fori_loop(1, heads, greet, 0)
    for n in range(1, planes):
        pl.semaphore_signal(
            barrier, inc=1, device_id=plane_peer(modulo(z + n, planes)), device_id_type=MESH
        )

    ends = []
    end = jnp.int32(0)
    for n in range(len_ref.shape[0]):
        end = end + len_ref[n]
        ends.append(end)

    def doc_of(where):
        return sum([(where >= e).astype(jnp.int32) for e in ends])

    def equal(a, b):
        return jnp.where(a == b, 1.0, 0.0).astype(F32)

    start = block * DH
    row_doc = doc_of(start + lax.broadcasted_iota(jnp.int32, (DH, DH), 0))
    rows_ref[1] = jnp.where(row_doc == doc_of(start + DH - 1), 1.0, 0.0).astype(F32)

    def owned(g):
        return g * per_group + my_head

    def slab_rows(s):
        return pl.ds(pl.multiple_of(s * slab, slab), slab)

    def remote(refs, sem, p):
        return pltpu.make_async_remote_copy(
            src_ref=refs[0],
            dst_ref=refs[1],
            send_sem=sem,
            recv_sem=refs[2],
            device_id=peer(p),
            device_id_type=MESH,
        )

    def send_states(way, g, a, own):
        for n in range(GROUPS):
            s = modulo(mine + n, GROUPS)
            source = state_out.at[way, g * per_group + a, slab_rows(s)]
            refs = source, state_in.at[way, g, mine], state_sem.at[way, g]
            if own and n == 0:
                pltpu.make_async_copy(*refs).start()
            else:
                remote(refs, send_sem.at[way, 0], a * GROUPS + s).start()

    def ahead(lap, j):
        return modulo(my_head + lap * UNROLL + j, per_group)

    def forward_states(g, lap):
        for j in range(UNROLL):
            h = g * per_group + ahead(lap, j)
            fk = feature(k_ref[:, cols(h)].astype(F32))
            fk_ref[h] = fk.astype(BF16)
            masked = (fk * rows_ref[1]).astype(BF16)
            state_out[0, h] = mm(masked, v_ref[:, cols(h)], 0, 0).astype(BF16)

    def forward_sends(g, lap):
        for j in range(UNROLL):
            send_states(0, g, ahead(lap, j), lap == 0 and j == 0)

    def local_forward(g):
        def lap(it, carry):
            for j in range(UNROLL):
                h = g * per_group + it * UNROLL + j
                fq = feature(q_ref[:, cols(h)].astype(F32)).astype(BF16)
                fq_ref[h] = fq
                scores = (mm(fq, fk_ref[h], 1, 1) * visible_ref[...]).astype(BF16)
                sc_ref[h] = scores
                att_ref[h] = mm(scores, v_ref[:, cols(h)], 1, 0)
            return carry

        lax.fori_loop(0, laps, lap, 0)

    def total_copy(way, g, n):
        target = modulo(z + n if way == 0 else z + planes - n, planes)
        return pltpu.make_async_remote_copy(
            src_ref=total_out.at[way, g],
            dst_ref=total_in.at[way, g, n - 1],
            send_sem=zsend_sem.at[way],
            recv_sem=zrecv_sem.at[way, g, n - 1],
            device_id=plane_peer(target),
            device_id_type=MESH,
        )

    def sum_up(way, g):
        pltpu.make_async_copy(state_in.at[way, g], state_in.at[way, g], state_sem.at[way, g]).wait()

        def add(n, total):
            for j in range(4):
                i = n * 4 + j
                total = total + state_in[way, g, i].astype(F32) * weight_ref[3 * way, i]
            return total

        total = lax.fori_loop(0, heads // 4, add, jnp.zeros((slab, DH), F32))
        total_out[way, g] = total.astype(BF16)
        for n in range(1, reach + 1):
            total_copy(way, g, n).start()

    def scan(way, g):
        run = jnp.zeros((slab, DH), F32)
        for n in range(1, reach + 1):
            total_copy(way, g, n).wait_recv()
            scale = zweight_ref[way, n - 1]
            run = run + total_in[way, g, n - 1].astype(F32) * scale

        def step(n, run):
            for j in range(4):
                i = n * 4 + j
                i = i if way == 0 else heads - 1 - i
                prefix_out[way, g, i] = (run * weight_ref[3 * way + 2, i]).astype(BF16)
                run = state_in[way, g, i].astype(F32) + run * weight_ref[3 * way + 1, i]
            return run

        lax.fori_loop(0, heads // 4, step, run)

        def refs(p):
            target = prefix_in.at[way, owned(g), slab_rows(my_slab)]
            return prefix_out.at[way, g, p], target, prefix_sem.at[way, owned(g)]

        pltpu.make_async_copy(*refs(mine)).start()
        for n in range(1, SPREAD):
            p = modulo(mine + n, heads)
            remote(refs(p), send_sem.at[way, 1], p).start()

        def spread(n, carry):
            for j in range(SPREAD):
                p = modulo(mine + n * SPREAD + j, heads)
                remote(refs(p), send_sem.at[way, 1], p).start()
            return carry

        lax.fori_loop(1, heads // SPREAD, spread, 0)

    def arrive(way, h):
        pltpu.make_async_copy(prefix_in.at[way, h], prefix_in.at[way, h], prefix_sem.at[way, h]).wait()

    def behind(lap, j):
        return modulo(my_head + per_group - lap * UNROLL - j, per_group)

    def attend_states(g, lap):
        spots = [behind(lap, j) for j in range(UNROLL)]
        for a in spots:
            arrive(0, g * per_group + a)
        for a in spots:
            h = g * per_group + a
            head_rows = rows_ref[0]
            fq = fq_ref[h]
            att = att_ref[h] + mm(fq, prefix_in[0, h], 1, 0) * head_rows
            inv = lax.rsqrt(jnp.mean(att * att, axis=-1, keepdims=True) + 1e-05)
            normed = att * inv
            o_ref[:, cols(h)] = normed.astype(BF16)
            grad = g_ref[:, cols(h)].astype(F32)
            mean = jnp.mean(grad * normed, axis=-1, keepdims=True)
            ga = ((grad - normed * mean) * inv).astype(BF16)
            ga_ref[h] = ga
            masked = (fq.astype(F32) * head_rows).astype(BF16)
            state_out[1, h] = mm(masked, ga, 0, 0).astype(BF16)

    def attend_sends(g, lap):
        for j in range(UNROLL):
            send_states(1, g, behind(lap, j), lap == 0 and j == 0)

    def local_back(g):
        def lap(it, carry):
            for j in range(UNROLL):
                h = g * per_group + it * UNROLL + j
                ga, fq, fk = ga_ref[h], fq_ref[h], fk_ref[h]
                grads = (mm(ga, v_ref[:, cols(h)], 1, 1) * visible_ref[...]).astype(BF16)
                gfq = mm(grads, fk, 1, 0) + mm(ga, prefix_in[0, h], 1, 1) * rows_ref[0]
                gq_ref[:, cols(h)] = (gfq * slope(q_ref[:, cols(h)].astype(F32))).astype(BF16)
                gfk_ref[h] = mm(grads, fq, 0, 0)
                gfv_ref[h] = mm(sc_ref[h], ga, 0, 0)
            return carry

        lax.fori_loop(0, laps, lap, 0)

    def finish_lap(g, it, carry):
        spots = [behind(it, j) for j in range(UNROLL)]
        for a in spots:
            arrive(1, g * per_group + a)
        for a in spots:
            h = g * per_group + a
            outgoing = prefix_in[1, h]
            gfk = gfk_ref[h] + mm(v_ref[:, cols(h)], outgoing, 1, 1) * rows_ref[1]
            gk_ref[:, cols(h)] = (gfk * slope(k_ref[:, cols(h)].astype(F32))).astype(BF16)
            gfv = gfv_ref[h] + mm(fk_ref[h], outgoing, 1, 0) * rows_ref[1]
            gv_ref[:, cols(h)] = gfv.astype(BF16)
        return carry

    def attend(g):
        for lap in range(laps + 1):
            if lap < laps:
                attend_states(g, lap)
            if lap > 0:
                attend_sends(g, lap - 1)

    def finish(g):
        lax.fori_loop(0, laps, functools.partial(finish_lap, g), 0)

    order = [(g, lap) for g in range(GROUPS) for lap in range(laps)]
    for n in range(len(order) + 1):
        if n < len(order):
            if order[n][1] == 0:
                for load in first_loads[order[n][0]]:
                    load.wait()
            forward_states(*order[n])
        if n == 1:
            pl.semaphore_wait(barrier, heads - 1 + planes - 1)
        if n > 0:
            forward_sends(*order[n - 1])
    for load in late_loads:
        load.start()

    col_doc = doc_of(start + lax.broadcasted_iota(jnp.int32, (DH, DH), 1))
    causal = lax.broadcasted_iota(jnp.int32, (DH, DH), 0) >= lax.broadcasted_iota(
        jnp.int32, (DH, DH), 1
    )
    visible_ref[...] = jnp.where(causal & (row_doc == col_doc), 1.0, 0.0).astype(F32)
    rows_ref[0] = jnp.where(row_doc == doc_of(start), 1.0, 0.0).astype(F32)

    plane_start = z * (heads * DH)
    plane_first = doc_of(plane_start)
    plane_last = doc_of(plane_start + heads * DH - 1)

    def weigh(i, carry):
        begin = plane_start + i * DH
        before, first = doc_of(begin - 1), doc_of(begin)
        last, after = doc_of(begin + DH - 1), doc_of(begin + DH)
        weight_ref[0, i] = equal(last, plane_last)
        weight_ref[1, i] = equal(last, before)
        weight_ref[2, i] = equal(first, before)
        weight_ref[3, i] = equal(first, plane_first)
        weight_ref[4, i] = equal(first, after)
        weight_ref[5, i] = equal(last, after)
        return carry

    lax.fori_loop(0, heads, weigh, 0)
    before_plane, after_plane = doc_of(plane_start - 1), doc_of(plane_start + heads * DH)
    for n in range(1, reach + 1):
        lower = equal(doc_of((z - n + 1) * (heads * DH) - 1), before_plane)
        upper = equal(doc_of((z + n) * (heads * DH)), after_plane)
        zweight_ref[0, n - 1] = jnp.where(z >= n, lower, 0.0)
        zweight_ref[1, n - 1] = jnp.where(z + n < planes, upper, 0.0)

    for load in late_loads:
        load.wait()
    steps = {
        "L": local_forward,
        "T": functools.partial(sum_up, 0),
        "P": functools.partial(scan, 0),
        "A": attend,
        "M": local_back,
        "U": functools.partial(sum_up, 1),
        "Q": functools.partial(scan, 1),
        "F": finish,
    }
    for n in range(0, len(SCHEDULE), 2):
        steps[SCHEDULE[n]](int(SCHEDULE[n + 1]))
    for way in range(2):
        for n in range(2):
            sent = state_out.at[way, pl.ds(0, heads - 1)]
            pltpu.make_async_copy(sent, sent, send_sem.at[way, n]).wait()
        for n in range(1, reach + 1):
            pltpu.make_async_copy(total_out.at[way], total_out.at[way], zsend_sem.at[way]).wait()


def write_out(*refs):
    sources, targets, sem = refs[:4], refs[4:8], refs[8]
    step = sources[0].shape[0] // WRITES
    copies = [
        pltpu.make_async_copy(
            sources[n].at[pl.ds(m * step, step)], targets[n].at[pl.ds(m * step, step)], sem.at[n, m]
        )
        for n in range(4)
        for m in range(WRITES)
    ]
    for copy in copies:
        copy.start()
    for copy in copies:
        copy.wait()


def solution(mesh):
    seq_axis, head_axis = mesh.shape["seq"], mesh.shape["head"]

    def local(queries, keys, values, out_grad, doc_lengths):
        rows, width = queries.shape
        heads = width // DH
        plane_seq = heads // head_axis
        planes = seq_axis // plane_seq
        reach = min(planes - 1, -(-DOC_MOST // (heads * DH)))
        cfg = (heads, plane_seq, head_axis, planes, reach)
        flat = [pltpu.VMEM((rows, width), BF16)] * 4
        per_head = [pltpu.VMEM((heads, DH, DH), BF16)] * 4
        wide = [pltpu.VMEM((heads, DH, DH), F32)] * 3
        out = jax.ShapeDtypeStruct((rows, width), BF16)
        hbm = pl.BlockSpec(memory_space=pl.ANY)
        parts = pl.pallas_call(
            functools.partial(kernel, cfg),
            out_shape=(pltpu.VMEM((rows, width), BF16),) * 4,
            in_specs=[pl.BlockSpec(memory_space=pltpu.SMEM)] + [hbm] * 4,
            out_specs=(pl.BlockSpec(memory_space=pltpu.VMEM),) * 4,
            scratch_shapes=flat
            + per_head
            + wide
            + [
                pltpu.VMEM((2, heads, DH, DH), BF16),
                pltpu.VMEM((2, GROUPS, heads, DH // GROUPS, DH), BF16),
                pltpu.VMEM((2, GROUPS, heads, DH // GROUPS, DH), BF16),
                pltpu.VMEM((2, heads, DH, DH), BF16),
                pltpu.VMEM((2, GROUPS, DH // GROUPS, DH), BF16),
                pltpu.VMEM((2, GROUPS, reach, DH // GROUPS, DH), BF16),
                pltpu.VMEM((DH, DH), F32),
                pltpu.VMEM((2, DH, DH), F32),
                pltpu.SMEM((6, heads), F32),
                pltpu.SMEM((2, reach), F32),
                pltpu.SemaphoreType.DMA((2, 2)),
                pltpu.SemaphoreType.DMA((2, GROUPS)),
                pltpu.SemaphoreType.DMA((2, heads)),
                pltpu.SemaphoreType.DMA((2,)),
                pltpu.SemaphoreType.DMA((2, GROUPS, reach)),
                pltpu.SemaphoreType.DMA((2 + 2 * GROUPS,)),
            ],
            compiler_params=pltpu.CompilerParams(
                collective_id=0, has_side_effects=True, vmem_limit_bytes=KERNEL_VMEM_KIB << 10
            ),
        )(doc_lengths, queries, keys, values, out_grad)
        return pl.pallas_call(
            write_out,
            out_shape=(out,) * 4,
            in_specs=[pl.BlockSpec(memory_space=pltpu.VMEM)] * 4,
            out_specs=(hbm,) * 4,
            scratch_shapes=[pltpu.SemaphoreType.DMA((4, WRITES))],
            compiler_params=pltpu.CompilerParams(vmem_limit_bytes=16 << 20),
        )(*parts)

    return jax.shard_map(
        local,
        mesh=mesh,
        in_specs=(P(("seq", "head"), None),) * 4 + (P(),),
        out_specs=(P(("seq", "head"), None),) * 4,
        check_vma=False,
    )
```

time: 70.3 us -> 68 us (0.967)
  Pallas kernels: 69.4 us -> 67.1 us
    pallas_call x1, Pallas kernels: 67.4 us -> 65.1 us  [local(): pl.pallas_call(functools.partial(kernel, cfg), out_shape=(pltpu.VMEM((row...]
where the time goes in v4:
time: 68 us; the launch traced here: 67.9 us
  Pallas kernels  67.1 us (99%)
  between operations  0.8 us (1%)
    pallas_call x1, Pallas kernels, local(): pl.pallas_call(functools.partial(kernel, cfg), out_shape=(pltpu.VMEM((row...  65.1 us
    pallas_call x1, Pallas kernels, local(): pl.pallas_call(write_out, out_shape=(out,) * 4, in_specs=[pl.BlockSpec(me...  2.04 us

profile of v4, /device:TPU:1, one launch (start us, length us, event | category | flops | bytes accessed | tf_op | source)
XLA Modules:
  0.0 67.9 jit_solution(1265808745361438417)
XLA Ops:
  0.6 65.1 %shard_map.84 = (bf16[128,4096]{1,0:T(8,128)(2,1)S(1)}, bf16[128,4096]{1,0:T(8,128)(2,1)S(1)}, bf16[128,4096]{1,0:T(8,128)(2,1)S(1)}, bf16[128,4096]{1,0:T(8,128)(2,1)S(1)}) custom-call(s32[8]{0:T(128)} %len_ref.1, bf16[128,4096]{1,0:T(8,128)(2,1)} %q_hbm.1, bf16[128,4096]{1,0:T(8,128)(2,1)} %k_hbm.1, bf16[128,4096]{1,0:T(8,128)(2,1)} %v_hbm.1, ...), custom_call_target="tpu_custom_call" | custom-call | tf_op jit(solution)/shard_map/pallas_call | solution.py:427
  65.7 2.0 %shard_map.85 = (bf16[128,4096]{1,0:T(8,128)(2,1)}, bf16[128,4096]{1,0:T(8,128)(2,1)}, bf16[128,4096]{1,0:T(8,128)(2,1)}, bf16[128,4096]{1,0:T(8,128)(2,1)}) custom-call(bf16[128,4096]{1,0:T(8,128)(2,1)S(1)} %get-tuple-element.8.refs_0_, bf16[128,4096]{1,0:T(8,128)(2,1)S(1)} %get-tuple-element.9.refs_1_, bf16[128,4096]{1,0:T(8,128)(2,1)S(1)} %get-tuple-element.10.refs_2_, ...), custom_call_target="tpu_custom_call" | custom-call | tf_op jit(solution)/shard_map/pallas_call | solution.py:457

commit v5 on v4

--- a/solution.py
+++ b/solution.py
@@ -56,6 +56,7 @@
     v_ref,
     g_ref,
     fq_ref,
+    fqm_ref,
     fk_ref,
     sc_ref,
     ga_ref,
@@ -192,8 +193,10 @@
         def lap(it, carry):
             for j in range(UNROLL):
                 h = g * per_group + it * UNROLL + j
-                fq = feature(q_ref[:, cols(h)].astype(F32)).astype(BF16)
+                wide = feature(q_ref[:, cols(h)].astype(F32))
+                fq = wide.astype(BF16)
                 fq_ref[h] = fq
+                fqm_ref[h] = (wide * rows_ref[0]).astype(BF16)
                 scores = (mm(fq, fk_ref[h], 1, 1) * visible_ref[...]).astype(BF16)
                 sc_ref[h] = scores
                 att_ref[h] = mm(scores, v_ref[:, cols(h)], 1, 0)
@@ -223,7 +226,7 @@
 
         total = lax.fori_loop(0, heads // 4, add, jnp.zeros((slab, DH), F32))
         total_out[way, g] = total.astype(BF16)
-        for n in range(1, reach + 1):
+        for n in range(reach, 0, -1):
             total_copy(way, g, n).start()
 
     def scan(way, g):
@@ -272,9 +275,8 @@
             arrive(0, g * per_group + a)
         for a in spots:
             h = g * per_group + a
-            head_rows = rows_ref[0]
-            fq = fq_ref[h]
-            att = att_ref[h] + mm(fq, prefix_in[0, h], 1, 0) * head_rows
+            masked = fqm_ref[h]
+            att = att_ref[h] + mm(masked, prefix_in[0, h], 1, 0)
             inv = lax.rsqrt(jnp.mean(att * att, axis=-1, keepdims=True) + 1e-05)
             normed = att * inv
             o_ref[:, cols(h)] = normed.astype(BF16)
@@ -282,7 +284,6 @@
             mean = jnp.mean(grad * normed, axis=-1, keepdims=True)
             ga = ((grad - normed * mean) * inv).astype(BF16)
             ga_ref[h] = ga
-            masked = (fq.astype(F32) * head_rows).astype(BF16)
             state_out[1, h] = mm(masked, ga, 0, 0).astype(BF16)
 
     def attend_sends(g, lap):
@@ -420,7 +421,7 @@
         reach = min(planes - 1, -(-DOC_MOST // (heads * DH)))
         cfg = (heads, plane_seq, head_axis, planes, reach)
         flat = [pltpu.VMEM((rows, width), BF16)] * 4
-        per_head = [pltpu.VMEM((heads, DH, DH), BF16)] * 4
+        per_head = [pltpu.VMEM((heads, DH, DH), BF16)] * 5
         wide = [pltpu.VMEM((heads, DH, DH), F32)] * 3
         out = jax.ShapeDtypeStruct((rows, width), BF16)
         hbm = pl.BlockSpec(memory_space=pl.ANY)

time: 68 us -> 67.4 us (level)
  no operation moved by 1% of the time
where the time goes in v5:
time: 67.4 us; the launch traced here: 67.3 us
  Pallas kernels  66.5 us (99%)
  between operations  0.8 us (1%)
    pallas_call x1, Pallas kernels, local(): pl.pallas_call(functools.partial(kernel, cfg), out_shape=(pltpu.VMEM((row...  64.5 us
    pallas_call x1, Pallas kernels, local(): pl.pallas_call(write_out, out_shape=(out,) * 4, in_specs=[pl.BlockSpec(me...  2.04 us

profile of v5, /device:TPU:1, one launch (start us, length us, event | category | flops | bytes accessed | tf_op | source)
XLA Modules:
  0.0 67.3 jit_solution(11943876164248230462)
XLA Ops:
  0.6 64.5 %shard_map.84 = (bf16[128,4096]{1,0:T(8,128)(2,1)S(1)}, bf16[128,4096]{1,0:T(8,128)(2,1)S(1)}, bf16[128,4096]{1,0:T(8,128)(2,1)S(1)}, bf16[128,4096]{1,0:T(8,128)(2,1)S(1)}) custom-call(s32[8]{0:T(128)} %len_ref.1, bf16[128,4096]{1,0:T(8,128)(2,1)} %q_hbm.1, bf16[128,4096]{1,0:T(8,128)(2,1)} %k_hbm.1, bf16[128,4096]{1,0:T(8,128)(2,1)} %v_hbm.1, ...), custom_call_target="tpu_custom_call" | custom-call | tf_op jit(solution)/shard_map/pallas_call | solution.py:428
  65.1 2.0 %shard_map.85 = (bf16[128,4096]{1,0:T(8,128)(2,1)}, bf16[128,4096]{1,0:T(8,128)(2,1)}, bf16[128,4096]{1,0:T(8,128)(2,1)}, bf16[128,4096]{1,0:T(8,128)(2,1)}) custom-call(bf16[128,4096]{1,0:T(8,128)(2,1)S(1)} %get-tuple-element.8.refs_0_, bf16[128,4096]{1,0:T(8,128)(2,1)S(1)} %get-tuple-element.9.refs_1_, bf16[128,4096]{1,0:T(8,128)(2,1)S(1)} %get-tuple-element.10.refs_2_, ...), custom_call_target="tpu_custom_call" | custom-call | tf_op jit(solution)/shard_map/pallas_call | solution.py:458

commit v6 on v5

--- a/solution.py
+++ b/solution.py
@@ -60,6 +60,9 @@
     fk_ref,
     sc_ref,
     ga_ref,
+    fkm_ref,
+    vm_ref,
+    slope_ref,
     att_ref,
     gfk_ref,
     gfv_ref,
@@ -183,6 +186,7 @@
             fk = feature(k_ref[:, cols(h)].astype(F32))
             fk_ref[h] = fk.astype(BF16)
             masked = (fk * rows_ref[1]).astype(BF16)
+            fkm_ref[h] = masked
             state_out[0, h] = mm(masked, v_ref[:, cols(h)], 0, 0).astype(BF16)
 
     def forward_sends(g, lap):
@@ -197,6 +201,8 @@
                 fq = wide.astype(BF16)
                 fq_ref[h] = fq
                 fqm_ref[h] = (wide * rows_ref[0]).astype(BF16)
+                vm_ref[h] = (v_ref[:, cols(h)].astype(F32) * rows_ref[1]).astype(BF16)
+                slope_ref[h] = slope(k_ref[:, cols(h)].astype(F32))
                 scores = (mm(fq, fk_ref[h], 1, 1) * visible_ref[...]).astype(BF16)
                 sc_ref[h] = scores
                 att_ref[h] = mm(scores, v_ref[:, cols(h)], 1, 0)
@@ -311,9 +317,9 @@
         for a in spots:
             h = g * per_group + a
             outgoing = prefix_in[1, h]
-            gfk = gfk_ref[h] + mm(v_ref[:, cols(h)], outgoing, 1, 1) * rows_ref[1]
-            gk_ref[:, cols(h)] = (gfk * slope(k_ref[:, cols(h)].astype(F32))).astype(BF16)
-            gfv = gfv_ref[h] + mm(fk_ref[h], outgoing, 1, 0) * rows_ref[1]
+            gfk = gfk_ref[h] + mm(vm_ref[h], outgoing, 1, 1)
+            gk_ref[:, cols(h)] = (gfk * slope_ref[h]).astype(BF16)
+            gfv = gfv_ref[h] + mm(fkm_ref[h], outgoing, 1, 0)
             gv_ref[:, cols(h)] = gfv.astype(BF16)
         return carry
 
@@ -432,6 +438,8 @@
             out_specs=(pl.BlockSpec(memory_space=pltpu.VMEM),) * 4,
             scratch_shapes=flat
             + per_head
+            + [pltpu.VMEM((heads, DH, DH), BF16)] * 2
+            + [pltpu.VMEM((heads, DH, DH), F32)]
             + wide
             + [
                 pltpu.VMEM((2, heads, DH, DH), BF16),

time: 67.4 us -> 67.4 us (level)
  no operation moved by 1% of the time
where the time goes in v6:
time: 67.4 us; the launch traced here: 66.9 us
  Pallas kernels  66.1 us (98%)
  between operations  0.8 us (1%)
    pallas_call x1, Pallas kernels, local(): pl.pallas_call(functools.partial(kernel, cfg), out_shape=(pltpu.VMEM((row...  64.1 us
    pallas_call x1, Pallas kernels, local(): pl.pallas_call(write_out, out_shape=(out,) * 4, in_specs=[pl.BlockSpec(me...  2.04 us

profile of v6, /device:TPU:1, one launch (start us, length us, event | category | flops | bytes accessed | tf_op | source)
XLA Modules:
  0.0 66.9 jit_solution(16138902627302573976)
XLA Ops:
  0.6 64.1 %shard_map.84 = (bf16[128,4096]{1,0:T(8,128)(2,1)S(1)}, bf16[128,4096]{1,0:T(8,128)(2,1)S(1)}, bf16[128,4096]{1,0:T(8,128)(2,1)S(1)}, bf16[128,4096]{1,0:T(8,128)(2,1)S(1)}) custom-call(s32[8]{0:T(128)} %len_ref.1, bf16[128,4096]{1,0:T(8,128)(2,1)} %q_hbm.1, bf16[128,4096]{1,0:T(8,128)(2,1)} %k_hbm.1, bf16[128,4096]{1,0:T(8,128)(2,1)} %v_hbm.1, ...), custom_call_target="tpu_custom_call" | custom-call | tf_op jit(solution)/shard_map/pallas_call | solution.py:434
  64.7 2.0 %shard_map.85 = (bf16[128,4096]{1,0:T(8,128)(2,1)}, bf16[128,4096]{1,0:T(8,128)(2,1)}, bf16[128,4096]{1,0:T(8,128)(2,1)}, bf16[128,4096]{1,0:T(8,128)(2,1)}) custom-call(bf16[128,4096]{1,0:T(8,128)(2,1)S(1)} %get-tuple-element.8.refs_0_, bf16[128,4096]{1,0:T(8,128)(2,1)S(1)} %get-tuple-element.9.refs_1_, bf16[128,4096]{1,0:T(8,128)(2,1)S(1)} %get-tuple-element.10.refs_2_, ...), custom_call_target="tpu_custom_call" | custom-call | tf_op jit(solution)/shard_map/pallas_call | solution.py:466
